TPU v7x, 256 devices: a whole 4x4x8 slice. The times are simulated.
256 devices in a mesh: space: 64 (over x, z, core), tpair: 4 (over y).
Axes of the slice: x: 4, y: 4, z: 8, core: 2. Of those that a mesh axis runs over, the one named last changes fastest.
Arguments:
- eigvecs: bfloat16 [4, 2, 3, 64, 8192], P('tpair', None, None, None, 'space'), may hold values from -6 to 6
- momenta: int32 [8, 3], replicated, may hold values from -2 to 2
- perams: bfloat16 [4, 4, 16, 2, 4096], P('tpair'), may hold values from -0.5 to 0.5
- sources: int32 [4], replicated, may hold values from 0 to 3, each once
- spins: int32 [2, 3, 2], replicated, may hold values from 0 to 3
Outputs:
- baryon: float32 [4, 4, 2, 512, 2, 4096], P('tpair', None, None, 'space')
Inputs may be any that keep to these rules, and one draw needn't show every extreme that they name: The entries of sources are distinct.
All inputs are finite; a program needn't handle non-finite values.
Results may differ from a plain program's by a relative error of at most 0.0064.
Values may be sent and summed in bfloat16 or wider, within the bound.
A program may use at most 128 MiB of HBM per device.

v0:
```python
import jax
import jax.numpy as jnp
from jax import lax
from jax.sharding import PartitionSpec as P

LEXT = 64


TWO_PI = 6.283185307179586


def every_cross(vecs):
    vfloat = vecs.astype(jnp.float32)
    pieces = []
    for colour in range(3):
        next_one = (colour + 1) % 3
        after_one = (colour + 2) % 3
        left_rn = vfloat[0, next_one][:, None, :]
        left_in = vfloat[1, next_one][:, None, :]
        left_ra = vfloat[0, after_one][:, None, :]
        left_ia = vfloat[1, after_one][:, None, :]
        right_rn = vfloat[0, next_one][None, :, :]
        right_in = vfloat[1, next_one][None, :, :]
        right_ra = vfloat[0, after_one][None, :, :]
        right_ia = vfloat[1, after_one][None, :, :]
        real_part = (
            left_rn * right_ra - left_in * right_ia - (left_ra * right_rn - left_ia * right_in)
        )
        imag_part = (
            left_rn * right_ia + left_in * right_ra - (left_ra * right_in + left_ia * right_rn)
        )
        pieces.append(jnp.stack([real_part, imag_part], axis=2).astype(jnp.bfloat16))
    return jnp.stack(pieces, axis=3)


def projected_left(block_vecs, momenta, offset, total_sites):
    site_count = block_vecs.shape[-1]
    site_ids = offset + jnp.arange(site_count, dtype=jnp.int32)
    coords = jnp.stack([site_ids % LEXT, site_ids // LEXT % LEXT, site_ids // (LEXT * LEXT)])
    turns = jnp.mod(jnp.sum(momenta[:, :, None] * coords[None, :, :], axis=1), LEXT)
    angle = turns.astype(jnp.float32) * (TWO_PI / LEXT)
    factor = lax.rsqrt(jnp.float32(24.0 * total_sites))
    cosine = (jnp.cos(angle) * factor)[:, None, None, :]
    sine = (jnp.sin(angle) * factor)[:, None, None, :]
    vfloat = block_vecs.astype(jnp.float32)
    left_real = cosine * vfloat[0][None] + sine * vfloat[1][None]
    left_imag = cosine * vfloat[1][None] - sine * vfloat[0][None]
    upper_half = jnp.stack([left_real, left_imag], axis=0)
    lower_half = jnp.stack([-left_imag, left_real], axis=0)
    stacked = jnp.stack([upper_half, lower_half], axis=0)
    mom_count = momenta.shape[0]
    vectors = block_vecs.shape[2]
    stacked = jnp.transpose(stacked, (0, 3, 5, 1, 2, 4)).reshape(
        6 * site_count, 2 * mom_count * vectors
    )
    return stacked.astype(jnp.bfloat16)


def complex_blocks(blocks):
    tau_real = blocks[..., 0, :, :]
    tau_imag = blocks[..., 1, :, :]
    upper_half = jnp.stack([tau_real, tau_imag], axis=-2)
    lower_half = jnp.stack([-tau_imag, tau_real], axis=-2)
    return jnp.stack([upper_half, lower_half], axis=-4)


def select_blocks(sink_perams, sources, spins, vectors):
    count_times = sink_perams.shape[0]
    pick_time = (sources[:, None] == jnp.arange(count_times, dtype=jnp.int32)[None, :]).astype(
        jnp.bfloat16
    )
    spin_code = spins[:, :, 0] * 4 + spins[:, :, 1]
    pick_spin = (spin_code[:, :, None] == jnp.arange(16, dtype=jnp.int32)).astype(jnp.bfloat16)
    chosen = jnp.einsum(
        "st,cqa,taxy->scqxy", pick_time, pick_spin, sink_perams, preferred_element_type=jnp.float32
    )
    return chosen.astype(jnp.bfloat16).reshape(
        sources.shape[0] * spins.shape[0], 3, 2, vectors, vectors
    )


def on_device(eigvecs, momenta, perams, sources, spins):
    vecs = eigvecs[0]
    vectors = vecs.shape[2]
    sites_here = vecs.shape[3]
    mom_count = momenta.shape[0]
    space_count = lax.axis_size("space")
    offset = lax.axis_index("space") * sites_here
    projected = projected_left(vecs, momenta, offset, sites_here * space_count)
    columns = every_cross(vecs).reshape(vectors * vectors, -1)
    summed = lax.psum_scatter(
        jnp.dot(columns, projected, preferred_element_type=jnp.float32),
        "space",
        scatter_dimension=0,
        tiled=True,
    )
    rounded = summed.astype(jnp.bfloat16).reshape(summed.shape[0], 2, mom_count, vectors)
    arrived = lax.all_to_all(perams, "tpair", split_axis=1, concat_axis=0, tiled=True)
    blocks = select_blocks(arrived[:, 0], sources, spins, vectors)
    ymats = complex_blocks(blocks)
    spread = jnp.einsum(
        "cwmi,swiox->somxc", rounded, ymats[:, 0], preferred_element_type=jnp.float32
    ).astype(jnp.bfloat16)
    count_sc = spread.shape[0]
    spread = spread.reshape(count_sc, 2, mom_count * vectors, summed.shape[0])
    whole = lax.all_to_all(spread, "space", split_axis=2, concat_axis=3, tiled=True)
    rows_here = whole.shape[2]
    whole = whole.reshape(count_sc, 2, rows_here, vectors, vectors)
    middle = jnp.einsum(
        "swpjk,swkox->spjox", whole, ymats[:, 2], preferred_element_type=jnp.float32
    ).astype(jnp.bfloat16)
    result = jnp.einsum(
        "spjwk,swjox->spoxk", middle, ymats[:, 1], preferred_element_type=jnp.float32
    )
    return result.reshape(1, sources.shape[0], spins.shape[0], rows_here, 2, vectors * vectors)


def solution(mesh):
    placed = (
        P("tpair", None, None, None, "space"),
        P(),
        P("tpair", None, None, None, None),
        P(),
        P(),
    )
    return jax.shard_map(
        on_device,
        mesh=mesh,
        in_specs=placed,
        out_specs=P("tpair", None, None, "space", None, None),
        check_vma=False,
    )
```

profile of v0, /device:TPU:1, one launch (start us, length us, event | category | flops | bytes accessed | tf_op | source)
XLA Modules:
  0.0 326.7 jit_solution(6589491947970539925)
XLA Ops:
  6.6 0.9 fusion.46
  7.5 3.4 %fusion.8 = (bf16[64,64,1,1,128]{4,1,0,3,2:T(8,128)(2,1)S(1)}, bf16[64,64,1,1,128]{4,1,0,3,2:T(8,128)(2,1)S(1)}, bf16[64,64,1,1,128]{4,1,0,3,2:T(8,128)(2,1)S(1)...) fusion(f32[64,128]{1,0:T(8,128)S(1)} %get-tuple-element.20, ...), kind=kLoop, calls=%fused_computation.21 | loop fusion | flops 25165824 | bytes 6488064 | tf_op jit(solution)/shard_map/stack | solution.py:32
  10.9 3.2 maximum_maximum_fusion
  14.1 12.2 %copy.68 = bf16[64,64,2,3,128]{4,3,2,1,0:T(4,128)(2,1)} copy(bf16[64,64,2,3,128]{4,1,0,3,2:T(8,128)(2,1)} %maximum_maximum_fusion) | data formatting | bytes 12582912 | tf_op jit(solution)/shard_map/stack | solution.py:33
  26.3 16.5 %reshape.415 = bf16[4096,768]{1,0:T(8,128)(2,1)} reshape(bf16[64,64,2,3,128]{4,3,2,1,0:T(4,128)(2,1)} %copy.68) | data formatting | bytes 12582912 | tf_op jit(solution)/shard_map/reshape | solution.py:90
  42.8 0.1 multiply_reduce_fusion
  43.0 0.1 copy.69
  43.1 0.9 fusion.16
  44.0 1.1 maximum_bitcast_fusion.1
  45.1 1.5 maximum_bitcast_fusion
  46.6 2.5 convert_element_type.74
  49.1 12.5 %fusion.47 = f32[4096,1024]{1,0:T(8,128)} fusion(bf16[4096,768]{1,0:T(8,128)(2,1)} %reshape.415, bf16[768,1024]{0,1:T(8,128)(2,1)} %convert_element_type.74), kind=kOutput, calls=%fused_computation.93 | convolution fusion | flops 6442450944 | bytes 24641536 | tf_op jit(solution)/shard_map/dot_general | solution.py:92
  61.7 5.0 %all-to-all-start = ((bf16[1,4,16,2,4096]{4,3,2,0,1:T(2,128)(2,1)}), bf16[1,4,16,2,4096]{4,3,2,0,1:T(2,128)(2,1)S(1)}, u32[]{:S(2)}, u32[]{:S(2)}) async-start(bf16[1,4,16,2,4096]{4,3,2,0,1:T(2,128)(2,1)} %bitcast.3), calls=%async_computation | async-start | bytes 2097152 | tf_op jit(solution)/shard_map/all_to_all | solution.py:98
  66.8 13.5 %all-to-all-done = bf16[1,4,16,2,4096]{4,3,2,0,1:T(2,128)(2,1)S(1)} async-done(((bf16[1,4,16,2,4096]{4,3,2,0,1:T(2,128)(2,1)}), bf16[1,4,16,2,4096]{4,3,2,0,1:T(2,128)(2,1)S(1)}, u32[]{:S(2)}, u32[]{:S(2)}) %all-to-all-start) | async-done | bytes 1048608 | tf_op jit(solution)/shard_map/all_to_all | solution.py:98
  80.3 1.2 convolution_bitcast_fusion
  81.5 0.5 fusion
  82.0 0.4 copy.64
  82.5 0.5 reshape.414
  83.0 0.2 copy.96
  83.3 0.2 copy.95
  83.5 0.2 maximum_bitcast_fusion.4
  83.8 167.5 %reduce-scatter.2.cloned.1.call-done = f32[64,1024]{1,0:T(8,128)} async-done(((f32[4096,1024]{1,0:T(8,128)}), f32[64,1024]{1,0:T(8,128)}) %reduce-scatter.2.cloned.1.call-update) | async-done | bytes 262160 | tf_op jit(solution)/shard_map/reduce_scatter | solution.py:91
  251.3 1.0 convert_element_type.75
  252.3 0.2 reshape.416
  252.5 0.7 bitcast_convert_fusion.1
  253.2 3.5 %copy.114 = bf16[8,2,512,64]{3,1,0,2:T(2,128)(2,1)} copy(bf16[8,2,512,64]{3,2,1,0:T(8,128)(2,1)S(1)} %bitcast.135) | data formatting | bytes 2097152 | tf_op jit(solution)/shard_map/reshape | solution.py:105
  256.7 5.2 %reshape.431 = bf16[64,2,4096]{2,1,0:T(2,128)(2,1)S(1)} reshape(bf16[512,8,2,64]{3,2,1,0:T(2,128)(2,1)} %bitcast.136) | data formatting | bytes 2097152
  261.9 40.3 %all_to_all.24 = bf16[64,2,4096]{2,1,0:T(2,128)(2,1)} all-to-all(bf16[64,2,4096]{2,1,0:T(2,128)(2,1)S(1)} %reshape.431), channel_id=1, replica_groups=mesh['space'=64,'tpair'=4] {'space'}, dimensions={0} | all-to-all | bytes 2097152 | tf_op jit(solution)/shard_map/all_to_all | solution.py:106
  302.1 5.8 %reshape.432 = bf16[512,8,2,64]{3,2,1,0:T(2,128)(2,1)} reshape(bf16[64,2,4096]{2,1,0:T(2,128)(2,1)} %all_to_all.24) | data formatting | bytes 2097152
  307.9 5.5 %convolution_bitcast_fusion.1 = f32[8,8,2,64,64]{4,3,1,2,0:T(8,128)} fusion(bf16[8,2,64,8,64]{4,1,0,3,2:T(2,128)(2,1)} %bitcast.137, bf16[8,3,1,64,2,64]{3,5,2,4,0,1:T(8,128)(2,1)S(1)} %get-tuple-element.10, bf16[8,3,1,64,2,64]{3,5,2,4,0,1:T(8,128)(2,1)S(1)} %get-tuple-element.9), kind=kOutput, calls=%fused_computation.6 | convolution fusion | flops 270008320 | bytes 6291456 | tf_op jit(solution)/shard_map/spjwk,swjox->spoxk/dot_general | solution.py:112
  313.4 3.5 %reshape.418 = f32[1,4,2,8,2,4096]{5,3,4,2,1,0:T(8,128)S(1)} reshape(f32[8,8,2,64,64]{4,3,1,2,0:T(8,128)} %convolution_bitcast_fusion.1) | data formatting | bytes 4194304 | tf_op jit(solution)/shard_map/reshape | solution.py:115
  316.9 3.0 copy.77
  (18 shorter events, 0.3 us)
Async XLA Ops:
  6.5 244.8 %reduce-scatter.2.cloned.1.call-start = ((), (), s32[]{:S(2)}) async-start(), calls=%async_computation.3 | async-start | bytes 17039360 | tf_op jit(solution)/shard_map/reduce_scatter | solution.py:91
  26.3 16.5 %copy-start.1 = (s32[8,3]{0,1:T(4,128)S(1)}, s32[8,3]{0,1:T(4,128)}, u32[]{:S(2)}) copy-start(s32[8,3]{0,1:T(4,128)} %param.6) | copy-start | bytes 292
  61.7 5.0 %copy-start = (s32[2,3,2]{1,2,0:T(2,128)S(1)}, s32[2,3,2]{1,2,0:T(2,128)}, u32[]{:S(2)}) copy-start(s32[2,3,2]{1,2,0:T(2,128)} %param.9) | copy-start | bytes 148
  61.7 19.8 %copy-start.2 = (s32[4]{0:T(128)S(1)}, s32[4]{0:T(128)}, u32[]{:S(2)}) copy-start(s32[4]{0:T(128)} %param.8) | copy-start | bytes 52
  61.7 18.5 %all-to-all-start = ((bf16[1,4,16,2,4096]{4,3,2,0,1:T(2,128)(2,1)}), bf16[1,4,16,2,4096]{4,3,2,0,1:T(2,128)(2,1)S(1)}, u32[]{:S(2)}, u32[]{:S(2)}) async-start(bf16[1,4,16,2,4096]{4,3,2,0,1:T(2,128)(2,1)} %bitcast.3), calls=%async_computation | async-start | bytes 2097152 | tf_op jit(solution)/shard_map/all_to_all | solution.py:98
Sparse Core Ops, SparseCore 0:
  61.8 189.4 reduce-scatter.1
where the time goes:
time: 328 us; the launch traced here: 327 us
  waiting for transfers between devices  181 us (55%)
  local copies, waits for them, and re-layouts  53.9 us (16%)
  blocking collectives  40.3 us (12%)
  matrix products  20.6 us (6%)
  between operations  13.6 us (4%)
  other arithmetic  12.4 us (4%)
  starting transfers between devices  5.02 us (2%)
    reduce_scatter x1, waiting for transfers between devices, on_device(): lax.psum_scatter(jnp.dot(columns, projected, preferred_element_type=jnp.f...  168 us
    all_to_all x1, blocking collectives, on_device(): lax.all_to_all(spread, 'space', split_axis=2, concat_axis=3, tiled=True)  40.3 us
    reshape x1, local copies, waits for them, and re-layouts, on_device(): columns = every_cross(vecs).reshape(vectors * vectors, -1)  16.5 us
    all_to_all x1, waiting for transfers between devices, on_device(): lax.all_to_all(perams, 'tpair', split_axis=1, concat_axis=0, tiled=True)  13.5 us
    dot_general x1, matrix products, on_device(): jnp.dot(columns, projected, preferred_element_type=jnp.float32)  12.5 us
    another operation x1, local copies, waits for them, and re-layouts, every_cross(): return jnp.stack(pieces, axis=3)  12.2 us
    unnamed x10, local copies, waits for them, and re-layouts  11.4 us
  transfers between devices with their start and end apart: 2, of which 2 were waited for; matrix products, arithmetic and copies ran while one was open for 1% of the time, Pallas kernels for 0%

commit v1 on v0

v1 whole, which is shorter than its diff:
```python
import jax
import jax.numpy as jnp
from jax import lax
from jax.experimental import pallas as pl
from jax.experimental.pallas import tpu as pltpu
from jax.sharding import PartitionSpec as P

LEXT = 64
TWO_PI = 6.283185307179586
MESH = pl.DeviceIdType.MESH

NX, NZ, NC = 4, 8, 2
NY = 4
HALF = NZ // 2


def place():
    index = lax.axis_index("space")
    return index // (NZ * NC), (index // NC) % NZ, index % NC


def at_space(x, z, c):
    return {"space": (x * NZ + z) * NC + c}


def elemental_kernel(
    vec_ref, mom_ref, per_ref, elem_ref, arrived_ref,
    cosines, sines, fields, vfloat, left, right, total, outbox, inbox, chunk, all_chunks,
    ring_send, ring_recv, pair_send, pair_recv, sum_send, sum_recv,
    share_send, share_recv, swap_send, swap_recv, per_send, per_recv, per_own, own_sem,
):
    x, z, c = place()
    y = lax.axis_index("tpair")
    zhalf, zz = z // HALF, z % HALF
    slot_q = zz * NC + c
    on_right = at_space(x, (z + 1) % NZ, c)
    on_left = at_space(x, (z + NZ - 1) % NZ, c)
    partner = at_space(x, z, 1 - c)
    across = [at_space((x + step) % NX, z, c) for step in range(1, NX)]
    along = [at_space(x, zhalf * HALF + (zz + step) % HALF, c) for step in range(1, HALF)]
    sinks = [{"tpair": (y + step) % NY} for step in range(1, NY)]

    barrier = pltpu.get_barrier_semaphore()
    greeted = [on_right, on_left, partner] + across + along + sinks
    for target in greeted:
        pl.semaphore_signal(barrier, inc=1, device_id=target, device_id_type=MESH)
    own = pltpu.make_async_copy(vec_ref, fields.at[0, 0], own_sem)
    own.start()
    pl.semaphore_wait(barrier, len(greeted))
    own.wait()

    def ring_copy(rel, colour, rightward):
        there = (rel + NZ - 1) % NZ if rightward else (rel + 1) % NZ
        return pltpu.make_async_remote_copy(
            src_ref=fields.at[0, rel, :, colour],
            dst_ref=fields.at[0, there, :, colour],
            send_sem=ring_send.at[there, colour],
            recv_sem=ring_recv.at[there, colour],
            device_id=on_right if rightward else on_left,
            device_id_type=MESH,
        )

    def ring_arrival(rel, colour):
        return pltpu.make_async_remote_copy(
            src_ref=fields.at[0, rel, :, colour],
            dst_ref=fields.at[0, rel, :, colour],
            send_sem=ring_send.at[rel, colour],
            recv_sem=ring_recv.at[rel, colour],
            device_id=on_right,
            device_id_type=MESH,
        )

    def pair_copy(rel, colour):
        return pltpu.make_async_remote_copy(
            src_ref=fields.at[0, rel, :, colour],
            dst_ref=fields.at[1, rel, :, colour],
            send_sem=pair_send.at[rel, colour],
            recv_sem=pair_recv.at[rel, colour],
            device_id=partner,
            device_id_type=MESH,
        )

    for colour in range(3):
        ring_copy(0, colour, True).start()
        ring_copy(0, colour, False).start()
        pair_copy(0, colour).start()

    per_copies = []
    for step in range(1, NY):
        other = (y + step) % NY
        copy = pltpu.make_async_remote_copy(
            src_ref=per_ref.at[other],
            dst_ref=arrived_ref.at[y],
            send_sem=per_send.at[step - 1],
            recv_sem=per_recv.at[step - 1],
            device_id=sinks[step - 1],
            device_id_type=MESH,
        )
        copy.start()
        per_copies.append(copy)
    per_local = pltpu.make_async_copy(per_ref.at[y], arrived_ref.at[y], per_own)
    per_local.start()

    def relay(place_in_order):
        rel = jnp.where(place_in_order % 2 == 1, NZ - (place_in_order + 1) // 2, place_in_order // 2)
        for colour in range(3):
            ring_arrival(rel, colour).wait_recv()

            @pl.when((place_in_order % 2 == 1) & (place_in_order < 7))
            def _():
                ring_copy(rel, colour, True).start()

            @pl.when((place_in_order % 2 == 0) & (place_in_order < 6))
            def _():
                ring_copy(rel, colour, False).start()

            pair_copy(rel, colour).start()

    row = lax.broadcasted_iota(jnp.int32, (NC * NZ, 128), 0)
    lane = lax.broadcasted_iota(jnp.int32, (NC * NZ, 128), 1)
    core = jnp.where(row < NZ, c, 1 - c)
    sites = ((x * NZ + ((z + row) & (NZ - 1))) * NC + core) * 128 + lane
    xs, ys, zs = sites & (LEXT - 1), (sites >> 6) & (LEXT - 1), sites >> 12
    factor = lax.rsqrt(jnp.float32(24.0 * 128 * NX * NZ * NC))
    for mom in range(4):
        mine = 2 * mom + zhalf
        turns = mom_ref[mine, 0] * xs + mom_ref[mine, 1] * ys + mom_ref[mine, 2] * zs
        angle = (turns & (LEXT - 1)).astype(jnp.float32) * (TWO_PI / LEXT)
        cosines[mom] = jnp.cos(angle) * factor
        sines[mom] = jnp.sin(angle) * factor

    total[...] = jnp.zeros_like(total)

    def contract(core_slot, rel):
        for part in range(2):
            for colour in range(3):
                values = fields[core_slot, rel, part, colour].astype(jnp.float32)
                vfloat[part, colour, 0:64] = values
                vfloat[part, colour, 64:128] = values
        for colour in range(3):
            nxt, aft = (colour + 1) % 3, (colour + 2) % 3
            for odd in range(2):
                rows = pl.ds(odd, 32, stride=2)
                lrn, lin = vfloat[0, nxt, rows], vfloat[1, nxt, rows]
                lra, lia = vfloat[0, aft, rows], vfloat[1, aft, rows]
                for group in range(4):
                    rows = pl.ds(1 + slot_q + 8 * group + odd, 32, stride=2)
                    rrn, rin = vfloat[0, nxt, rows], vfloat[1, nxt, rows]
                    rra, ria = vfloat[0, aft, rows], vfloat[1, aft, rows]
                    real = lrn * rra - lin * ria - (lra * rrn - lia * rin)
                    imag = lrn * ria + lin * rra - (lra * rin + lia * rrn)
                    where = pl.ds(group * 64 + odd * 32, 32)
                    left[where, colour * 128 : (colour + 1) * 128] = real.astype(jnp.bfloat16)
                    left[where, (3 + colour) * 128 : (4 + colour) * 128] = imag.astype(jnp.bfloat16)
        at = pl.ds(core_slot * NZ + rel, 1)
        for colour in range(3):
            for odd in range(2):
                rows = pl.ds(odd, 32, stride=2)
                vr, vi = vfloat[0, colour, rows], vfloat[1, colour, rows]
                for mom in range(4):
                    cosine, sine = cosines[mom, at, :], sines[mom, at, :]
                    pr = (cosine * vr + sine * vi).astype(jnp.bfloat16)
                    pi = (cosine * vi - sine * vr).astype(jnp.bfloat16)
                    upper, lower = pl.ds(mom * 128 + odd * 32, 32), pl.ds(mom * 128 + 64 + odd * 32, 32)
                    first, second = pl.ds(colour * 128, 128), pl.ds((3 + colour) * 128, 128)
                    right[upper, first] = pr
                    right[upper, second] = -pi
                    right[lower, first] = pi
                    right[lower, second] = pr
        product = lax.dot_general(
            left[...], right[...], (((1,), (1,)), ((), ())), preferred_element_type=jnp.float32
        )
        for mom in range(4):
            total[mom] += product[:, mom * 128 : (mom + 1) * 128]

    relay(1)
    relay(2)

    def body(n, carry):
        rel = jnp.where(n % 2 == 1, NZ - (n + 1) // 2, n // 2)

        @pl.when((n >= 1) & (n < 6))
        def _():
            relay(n + 2)

        contract(0, rel)
        for colour in range(3):
            pair_copy(rel, colour).wait_recv()
        contract(1, rel)
        return carry

    lax.fori_loop(0, NZ, body, 0)

    sum_copies = []
    for step in (2, 1, 3):
        outbox[step - 1] = total[(x + step) % NX].astype(jnp.bfloat16)
        copy = pltpu.make_async_remote_copy(
            src_ref=outbox.at[step - 1],
            dst_ref=inbox.at[step - 1],
            send_sem=sum_send.at[step - 1],
            recv_sem=sum_recv.at[step - 1],
            device_id=across[step - 1],
            device_id_type=MESH,
        )
        copy.start()
        sum_copies.append(copy)
    for copy in sum_copies:
        copy.wait_recv()
    summed = total[x]
    for step in range(3):
        summed = summed + inbox[step].astype(jnp.float32)
    chunk[...] = summed.astype(jnp.bfloat16)

    def swap_copy(source, step):
        owner = (zz + NX - step) % HALF
        return pltpu.make_async_remote_copy(
            src_ref=source,
            dst_ref=all_chunks.at[owner * NC + c],
            send_sem=swap_send.at[step],
            recv_sem=swap_recv.at[step],
            device_id=partner,
            device_id_type=MESH,
        )

    share_copies = []
    for step in (3, 2, 1):
        copy = pltpu.make_async_remote_copy(
            src_ref=chunk,
            dst_ref=all_chunks.at[slot_q],
            send_sem=share_send.at[step - 1],
            recv_sem=share_recv.at[step - 1],
            device_id=along[step - 1],
            device_id_type=MESH,
        )
        copy.start()
        share_copies.append((step, copy))
    swap_copies = [swap_copy(chunk, 0)]
    swap_copies[0].start()
    elem_ref[slot_q] = chunk[...]
    for step, copy in reversed(share_copies):
        owner = (zz + HALF - step) % HALF
        arrival = pltpu.make_async_remote_copy(
            src_ref=chunk,
            dst_ref=all_chunks.at[owner * NC + c],
            send_sem=share_send.at[step - 1],
            recv_sem=share_recv.at[step - 1],
            device_id=along[step - 1],
            device_id_type=MESH,
        )
        arrival.wait_recv()
        onward = swap_copy(all_chunks.at[owner * NC + c], step)
        onward.start()
        swap_copies.append(onward)
        elem_ref[owner * NC + c] = all_chunks[owner * NC + c]
    for step in range(HALF):
        owner = (zz + HALF - step) % HALF
        theirs = owner * NC + 1 - c
        pltpu.make_async_remote_copy(
            src_ref=chunk,
            dst_ref=all_chunks.at[theirs],
            send_sem=swap_send.at[step],
            recv_sem=swap_recv.at[step],
            device_id=partner,
            device_id_type=MESH,
        ).wait_recv()
        elem_ref[theirs] = all_chunks[theirs]

    for rel in range(NZ):
        for colour in range(3):
            if rel in (7, 6, 5, 4):
                ring_copy((rel + 1) % NZ, colour, True).wait_send()
            elif rel:
                ring_copy(rel - 1, colour, False).wait_send()
            pair_copy(rel, colour).wait_send()
    for copy in sum_copies:
        copy.wait_send()
    for _, copy in share_copies:
        copy.wait_send()
    for copy in swap_copies:
        copy.wait_send()
    per_local.wait()
    for step, copy in enumerate(per_copies, 1):
        copy.wait_send()
        pltpu.make_async_remote_copy(
            src_ref=per_ref.at[y],
            dst_ref=arrived_ref.at[(y + NY - step) % NY],
            send_sem=per_send.at[step - 1],
            recv_sem=per_recv.at[step - 1],
            device_id=sinks[step - 1],
            device_id_type=MESH,
        ).wait_recv()


def elementals(vecs, momenta, perams):
    vmem = pl.BlockSpec(memory_space=pltpu.VMEM)
    anyspace = pl.BlockSpec(memory_space=pl.ANY)
    dma, bf16, f32 = pltpu.SemaphoreType.DMA, jnp.bfloat16, jnp.float32
    return pl.pallas_call(
        elemental_kernel,
        out_shape=(
            jax.ShapeDtypeStruct((8, 256, 128), bf16),
            jax.ShapeDtypeStruct(perams.shape, bf16),
        ),
        in_specs=[vmem, pl.BlockSpec(memory_space=pltpu.SMEM), anyspace],
        out_specs=(vmem, anyspace),
        scratch_shapes=[
            pltpu.VMEM((4, NC * NZ, 128), f32),
            pltpu.VMEM((4, NC * NZ, 128), f32),
            pltpu.VMEM((NC, NZ, 2, 3, 64, 128), bf16),
            pltpu.VMEM((2, 3, 128, 128), f32),
            pltpu.VMEM((256, 768), bf16),
            pltpu.VMEM((512, 768), bf16),
            pltpu.VMEM((4, 256, 128), f32),
            pltpu.VMEM((3, 256, 128), bf16),
            pltpu.VMEM((3, 256, 128), bf16),
            pltpu.VMEM((256, 128), bf16),
            pltpu.VMEM((8, 256, 128), bf16),
            dma((NZ, 3)), dma((NZ, 3)), dma((NZ, 3)), dma((NZ, 3)),
            dma((3,)), dma((3,)), dma((3,)), dma((3,)), dma((4,)), dma((4,)),
            dma((3,)), dma((3,)), dma(()), dma(()),
        ],
        compiler_params=pltpu.CompilerParams(collective_id=0, has_side_effects=True),
    )(vecs, momenta, perams)


def contract_kernel(
    sources_ref, spins_ref, elem_ref, arrived_ref, out_ref, full, rows, second, wide, tau0, first_op
):
    sn = pl.program_id(0)
    low = lax.broadcasted_iota(jnp.int32, (32, 128), 1) < 64
    even = lax.broadcasted_iota(jnp.int32, (32, 128), 1) % 2 == 0

    def tau(which, quark):
        source, comb = sources_ref[which // 2], which % 2
        spin = spins_ref[comb, quark, 0] * 4 + spins_ref[comb, quark, 1]
        flat = arrived_ref[source, spin].astype(jnp.float32)
        for pair in range(32):
            wide[2 * pair : 2 * pair + 2, :] = flat[:, pair * 128 : (pair + 1) * 128]
        return wide[pl.ds(0, 32, stride=2), :], wide[pl.ds(1, 32, stride=2), :]

    def rolled(value):
        return pltpu.roll(value, 64, 1)

    @pl.when(sn == 0)
    def _():
        full[pl.ds(0, 32, stride=129), :] = jnp.zeros((32, 128), jnp.float32)
        full[pl.ds(96, 32, stride=129), :] = jnp.zeros((32, 128), jnp.float32)
        for q in range(8):
            for group in range(4):
                d = 1 + q + 8 * group
                for odd in range(2):
                    at = group * 64 + odd * 32
                    piece = elem_ref[q, at : at + 32, :].astype(jnp.float32)
                    kodd = (odd + d) % 2
                    e = (odd + d - kodd) // 2
                    base = odd * 64 + kodd * 32 + e
                    full[pl.ds(base, 32 - e, stride=129), :] = piece[: 32 - e]
                    if e:
                        full[pl.ds(129 * (32 - e) + base - 32, e, stride=129), :] = piece[32 - e :]
                    if d < 32:
                        base = 128 * e + kodd * 64 + odd * 32
                        full[pl.ds(base, 32 - e, stride=129), :] = -piece[: 32 - e]
                        if e:
                            full[pl.ds(129 * (32 - e) + base - 4096, e, stride=129), :] = -piece[32 - e :]

        def load_tau0(which, carry):
            real, imag = tau(which, 0)
            upper = jnp.concatenate([real, rolled(real), -imag, -rolled(imag)], axis=0)
            lower = jnp.concatenate([rolled(imag), imag, rolled(real), real], axis=0)
            lanes = lax.broadcasted_iota(jnp.int32, (128, 128), 1)
            tau0[which] = jnp.where(lanes < 64, upper, lower).astype(jnp.bfloat16)
            return carry

        lax.fori_loop(0, 8, load_tau0, 0)
        mine = lax.axis_index("space") % 8
        row = lax.broadcasted_iota(jnp.int32, (16, 128), 0)
        lane = lax.broadcasted_iota(jnp.int32, (16, 128), 1)
        pick = (lane == (row // 8) * 64 + mine * 8 + row % 8).astype(jnp.float32).astype(jnp.bfloat16)
        for which in range(8):
            picked = lax.dot_general(
                pick, tau0[which], (((1,), (1,)), ((), ())), preferred_element_type=jnp.float32
            )
            for part in range(2):
                at = part * 64 + which * 8
                first_op[at : at + 8, :] = picked[part * 8 : part * 8 + 8]
        operator = first_op[...].astype(jnp.bfloat16)
        for p in range(32):
            block = full[p * 128 : (p + 1) * 128, :].astype(jnp.bfloat16)
            first = lax.dot_general(
                operator, block, (((1,), (1,)), ((), ())), preferred_element_type=jnp.float32
            )
            for part in range(2):
                for which in range(8):
                    at = part * 64 + which * 8
                    rows[which, p * 8 : (p + 1) * 8, part * 128 : (part + 1) * 128] = first[at : at + 8]

    real, imag = tau(sn, 2)

    def both_of_pair(value):
        turned, zero = rolled(value), jnp.zeros_like(value)
        return jnp.concatenate(
            [
                jnp.where(low, value, zero),
                jnp.where(low, turned, zero),
                jnp.where(low, zero, turned),
                jnp.where(low, zero, value),
            ],
            axis=0,
        ).astype(jnp.bfloat16)

    kreal, kimag = both_of_pair(real), both_of_pair(imag)
    operand2 = jnp.concatenate(
        [
            jnp.concatenate([kreal, kimag], axis=1),
            jnp.concatenate([-kimag, kreal], axis=1),
        ],
        axis=0,
    )
    product = jnp.dot(rows[sn].astype(jnp.bfloat16), operand2, preferred_element_type=jnp.float32)
    for part in range(2):
        second[part] = product[:, part * 128 : (part + 1) * 128]

    real, imag = tau(sn, 1)

    def arranged(upper, lower):
        uturn, lturn = rolled(upper), rolled(lower)
        straight = jnp.where(low, jnp.where(even, upper, uturn), jnp.where(even, lturn, lower))
        turned = jnp.where(low, jnp.where(even, uturn, upper), jnp.where(even, lower, lturn))
        return [straight, turned]

    operator1 = jnp.concatenate(arranged(real, imag) + arranged(-imag, real), axis=0).astype(jnp.bfloat16)
    row = lax.broadcasted_iota(jnp.int32, (128, 128), 0)
    lane = lax.broadcasted_iota(jnp.int32, (128, 128), 1)
    wanted = (row % 2) * 64 + 2 * (row % 64 // 2) + row // 64
    order = (lane == wanted).astype(jnp.float32).astype(jnp.bfloat16)
    t1 = lax.dot_general(
        order, operator1, (((1,), (1,)), ((), ())), preferred_element_type=jnp.float32
    ).astype(jnp.bfloat16)
    keep = lax.broadcasted_iota(jnp.int32, (64, 128), 1) < 64
    for i in range(8):
        parts = []
        for part in range(2):
            straight = second[part, pl.ds(i, 32, stride=8), :]
            parts += [straight, rolled(straight)]
        operand = jnp.concatenate(parts, axis=0).astype(jnp.bfloat16)
        both = jnp.dot(t1, operand, preferred_element_type=jnp.float32)
        out_ref[i] = jnp.where(keep, both[:64], both[64:])


def contractions(elem, arrived, sources, spins):
    return pl.pallas_call(
        contract_kernel,
        out_shape=jax.ShapeDtypeStruct((64, 64, 128), jnp.float32),
        grid_spec=pltpu.PrefetchScalarGridSpec(
            num_scalar_prefetch=2,
            grid=(8,),
            in_specs=[
                pl.BlockSpec((8, 256, 128), lambda s, *_: (0, 0, 0)),
                pl.BlockSpec((4, 16, 2, 4096), lambda s, *_: (0, 0, 0, 0)),
            ],
            out_specs=pl.BlockSpec((8, 64, 128), lambda s, *_: (s, 0, 0)),
            scratch_shapes=[
                pltpu.VMEM((4096, 128), jnp.float32),
                pltpu.VMEM((8, 256, 256), jnp.float32),
                pltpu.VMEM((2, 256, 128), jnp.float32),
                pltpu.VMEM((64, 128), jnp.float32),
                pltpu.VMEM((8, 128, 128), jnp.bfloat16),
                pltpu.VMEM((128, 128), jnp.float32),
            ],
        ),
        compiler_params=pltpu.CompilerParams(dimension_semantics=("arbitrary",)),
    )(sources, spins, elem, arrived)


def on_device(eigvecs, momenta, perams, sources, spins):
    elem, arrived = elementals(eigvecs[0], momenta, perams[0])
    result = contractions(elem, arrived, sources, spins)
    result = jnp.transpose(result.reshape(64, 32, 2, 128), (0, 2, 1, 3))
    return result.reshape(1, 4, 2, 8, 2, 4096)


def solution(mesh):
    placed = (
        P("tpair", None, None, None, "space"),
        P(),
        P("tpair", None, None, None, None),
        P(),
        P(),
    )
    return jax.shard_map(
        on_device,
        mesh=mesh,
        in_specs=placed,
        out_specs=P("tpair", None, None, "space", None, None),
        check_vma=False,
    )
```

time: 328 us -> 55.2 us (0.17)
  waiting for transfers between devices: 181 us -> 0 us
  Pallas kernels: 0 us -> 52.2 us
  local copies, waits for them, and re-layouts: 53.9 us -> 2.71 us
  blocking collectives: 40.3 us -> 0 us
  matrix products: 20.6 us -> 0 us
  between operations: 13.6 us -> 0.01 us
  other arithmetic: 12.4 us -> 0 us
  starting transfers between devices: 5.02 us -> 0 us
    reduce_scatter x1 -> x0, waiting for transfers between devices: 168 us -> none  [on_device(): lax.psum_scatter(jnp.dot(columns, projected, preferred_element_type=jnp.f...]
    pallas_call x0 -> x2, Pallas kernels: none -> 52.2 us  [the longest x1 42.1 us: elementals(): pl.pallas_call(elemental_kernel, out_shape=(jax.ShapeDtypeStruct((8, 256,...]
    all_to_all x1 -> x0, blocking collectives: 40.3 us -> none  [on_device(): lax.all_to_all(spread, 'space', split_axis=2, concat_axis=3, tiled=True)]
    reshape x6 -> x0, local copies, waits for them, and re-layouts: 27.1 us -> none  [the longest x1 16.5 us: on_device(): columns = every_cross(vecs).reshape(vectors * vectors, -1)]
    dot_general x5 -> x0, matrix products: 20.6 us -> none  [the longest x1 12.5 us: on_device(): jnp.dot(columns, projected, preferred_element_type=jnp.float32)]
    all_to_all x1 -> x0, waiting for transfers between devices: 13.5 us -> none  [on_device(): lax.all_to_all(perams, 'tpair', split_axis=1, concat_axis=0, tiled=True)]
    another operation x1 -> x0, local copies, waits for them, and re-layouts: 12.2 us -> none  [every_cross(): return jnp.stack(pieces, axis=3)]
    another operation x6 -> x0, other arithmetic: 8.8 us -> none  [the longest x1 3.38 us: every_cross(): jnp.stack([real_part, imag_part], axis=2).astype(jnp.bfloat16)]
  transfers between devices with their start and end apart: 2 -> 0, of which waited for: 2 -> 0; matrix products, arithmetic and copies ran while one was open for 1% -> 0% of each run, Pallas kernels for 0% -> 0%
where the time goes in v1:
time: 55.2 us; the launch traced here: 55 us
  Pallas kernels  52.2 us (95%)
  local copies, waits for them, and re-layouts  2.71 us (5%)
    pallas_call x1, Pallas kernels, elementals(): pl.pallas_call(elemental_kernel, out_shape=(jax.ShapeDtypeStruct((8, 256,...  42.1 us
    pallas_call x1, Pallas kernels, contractions(): pl.pallas_call(contract_kernel, out_shape=jax.ShapeDtypeStruct((64, 64, 1...  10.1 us
    unnamed x2, local copies, waits for them, and re-layouts  2.71 us

profile of v1, /device:TPU:1, one launch (start us, length us, event | category | flops | bytes accessed | tf_op | source)
XLA Modules:
  0.0 55.0 jit_solution(899058486586376506)
XLA Ops:
  0.0 1.3 %copy.6.mom_ref = s32[8,3]{1,0:T(8,128)} copy(s32[8,3]{0,1:T(4,128)} %param.6) | data formatting | bytes 192 | tf_op args[1]
  1.3 1.4 %copy.7.spins_ref = s32[2,3,2]{2,1,0:T(4,128)} copy(s32[2,3,2]{1,2,0:T(2,128)} %param.9) | data formatting | bytes 96 | tf_op args[4]
  2.7 42.1 %shard_map.55 = (bf16[8,256,128]{2,1,0:T(8,128)(2,1)}, bf16[4,16,2,4096]{3,2,1,0:T(2,128)(2,1)}) custom-call(bf16[2,3,64,128]{3,2,1,0:T(8,128)(2,1)} %bitcast.8, s32[8,3]{1,0:T(8,128)} %copy.6.mom_ref, bf16[4,16,2,4096]{3,2,1,0:T(2,128)(2,1)} %bitcast.7), custom_call_target="tpu_custom_call" | custom-call | tf_op jit(solution)/shard_map/pallas_call | solution.py:298
  44.9 10.1 %shard_map.56 = f32[64,64,128]{2,1,0:T(8,128)} custom-call(s32[4]{0:T(128)} %sources_ref.1, s32[2,3,2]{2,1,0:T(4,128)} %copy.7.spins_ref, bf16[8,256,128]{2,1,0:T(8,128)(2,1)} %get-tuple-element.7.elem_ref, bf16[4,16,2,4096]{3,2,1,0:T(2,128)(2,1)} %get-tuple-element.8.arrived_ref), custom_call_target="tpu_custom_call" | custom-call | tf_op jit(solution)/shard_map/pallas_call | solution.py:451

commit v2 on v1

v2 whole, which is shorter than its diff:
```python
import jax
import jax.numpy as jnp
from jax import lax
from jax.experimental import pallas as pl
from jax.experimental.pallas import tpu as pltpu
from jax.sharding import PartitionSpec as P

LEXT = 64
TWO_PI = 6.283185307179586
MESH = pl.DeviceIdType.MESH

NX, NZ, NC = 4, 8, 2
NY = 4
HALF = NZ // 2


def place():
    index = lax.axis_index("space")
    return index // (NZ * NC), (index // NC) % NZ, index % NC


def at_space(x, z, c):
    return {"space": (x * NZ + z) * NC + c}


def elemental_kernel(
    vec_ref, mom_ref, sources_ref, spins_ref, per_ref, rows_ref, second_op_ref, third_op_ref,
    cosines, sines, fields, vfloat, left, right, total, outbox, inbox, chunk, all_chunks,
    arrived, wide, full, first_op, ring_send, ring_recv, pair_send, pair_recv, sum_send, sum_recv,
    share_send, share_recv, swap_send, swap_recv, per_send, per_recv, per_own, own_sem,
):
    x, z, c = place()
    y = lax.axis_index("tpair")
    zhalf, zz = z // HALF, z % HALF
    slot_q = zz * NC + c
    on_right = at_space(x, (z + 1) % NZ, c)
    on_left = at_space(x, (z + NZ - 1) % NZ, c)
    partner = at_space(x, z, 1 - c)
    across = [at_space((x + step) % NX, z, c) for step in range(1, NX)]
    along = [at_space(x, zhalf * HALF + (zz + step) % HALF, c) for step in range(1, HALF)]
    sinks = [{"tpair": (y + step) % NY} for step in range(1, NY)]

    barrier = pltpu.get_barrier_semaphore()
    greeted = [on_right, on_left, partner] + across + along + sinks
    for target in greeted:
        pl.semaphore_signal(barrier, inc=1, device_id=target, device_id_type=MESH)
    own = pltpu.make_async_copy(vec_ref, fields.at[0, 0], own_sem)
    own.start()
    pl.semaphore_wait(barrier, len(greeted))
    own.wait()

    def ring_copy(rel, colour, rightward):
        there = (rel + NZ - 1) % NZ if rightward else (rel + 1) % NZ
        return pltpu.make_async_remote_copy(
            src_ref=fields.at[0, rel, :, colour],
            dst_ref=fields.at[0, there, :, colour],
            send_sem=ring_send.at[there, colour],
            recv_sem=ring_recv.at[there, colour],
            device_id=on_right if rightward else on_left,
            device_id_type=MESH,
        )

    def ring_arrival(rel, colour):
        return pltpu.make_async_remote_copy(
            src_ref=fields.at[0, rel, :, colour],
            dst_ref=fields.at[0, rel, :, colour],
            send_sem=ring_send.at[rel, colour],
            recv_sem=ring_recv.at[rel, colour],
            device_id=on_right,
            device_id_type=MESH,
        )

    def pair_copy(rel, colour):
        return pltpu.make_async_remote_copy(
            src_ref=fields.at[0, rel, :, colour],
            dst_ref=fields.at[1, rel, :, colour],
            send_sem=pair_send.at[rel, colour],
            recv_sem=pair_recv.at[rel, colour],
            device_id=partner,
            device_id_type=MESH,
        )

    for colour in range(3):
        ring_copy(0, colour, True).start()
        ring_copy(0, colour, False).start()
        pair_copy(0, colour).start()

    per_copies = []
    for step in range(1, NY):
        other = (y + step) % NY
        copy = pltpu.make_async_remote_copy(
            src_ref=per_ref.at[other],
            dst_ref=arrived.at[y],
            send_sem=per_send.at[step - 1],
            recv_sem=per_recv.at[step - 1],
            device_id=sinks[step - 1],
            device_id_type=MESH,
        )
        copy.start()
        per_copies.append(copy)
    per_local = pltpu.make_async_copy(per_ref.at[y], arrived.at[y], per_own)
    per_local.start()

    def relay(place_in_order):
        rel = jnp.where(place_in_order % 2 == 1, NZ - (place_in_order + 1) // 2, place_in_order // 2)
        for colour in range(3):
            ring_arrival(rel, colour).wait_recv()

            @pl.when((place_in_order % 2 == 1) & (place_in_order < 7))
            def _():
                ring_copy(rel, colour, True).start()

            @pl.when((place_in_order % 2 == 0) & (place_in_order < 6))
            def _():
                ring_copy(rel, colour, False).start()

            pair_copy(rel, colour).start()

    row = lax.broadcasted_iota(jnp.int32, (NC * NZ, 128), 0)
    lane = lax.broadcasted_iota(jnp.int32, (NC * NZ, 128), 1)
    core = jnp.where(row < NZ, c, 1 - c)
    sites = ((x * NZ + ((z + row) & (NZ - 1))) * NC + core) * 128 + lane
    xs, ys, zs = sites & (LEXT - 1), (sites >> 6) & (LEXT - 1), sites >> 12
    factor = lax.rsqrt(jnp.float32(24.0 * 128 * NX * NZ * NC))
    for mom in range(4):
        mine = 2 * mom + zhalf
        turns = mom_ref[0, mine] * xs + mom_ref[1, mine] * ys + mom_ref[2, mine] * zs
        angle = (turns & (LEXT - 1)).astype(jnp.float32) * (TWO_PI / LEXT)
        cosines[mom] = jnp.cos(angle) * factor
        sines[mom] = jnp.sin(angle) * factor

    total[...] = jnp.zeros_like(total)

    def contract(core_slot, rel):
        for part in range(2):
            for colour in range(3):
                values = fields[core_slot, rel, part, colour].astype(jnp.float32)
                vfloat[part, colour, 0:64] = values
                vfloat[part, colour, 64:128] = values
        for colour in range(3):
            nxt, aft = (colour + 1) % 3, (colour + 2) % 3
            for odd in range(2):
                rows = pl.ds(odd, 32, stride=2)
                lrn, lin = vfloat[0, nxt, rows], vfloat[1, nxt, rows]
                lra, lia = vfloat[0, aft, rows], vfloat[1, aft, rows]
                for group in range(4):
                    rows = pl.ds(1 + slot_q + 8 * group + odd, 32, stride=2)
                    rrn, rin = vfloat[0, nxt, rows], vfloat[1, nxt, rows]
                    rra, ria = vfloat[0, aft, rows], vfloat[1, aft, rows]
                    real = lrn * rra - lin * ria - (lra * rrn - lia * rin)
                    imag = lrn * ria + lin * rra - (lra * rin + lia * rrn)
                    where = pl.ds(group * 64 + odd * 32, 32)
                    left[where, colour * 128 : (colour + 1) * 128] = real.astype(jnp.bfloat16)
                    left[where, (3 + colour) * 128 : (4 + colour) * 128] = imag.astype(jnp.bfloat16)
        at = pl.ds(core_slot * NZ + rel, 1)
        for colour in range(3):
            for odd in range(2):
                rows = pl.ds(odd, 32, stride=2)
                vr, vi = vfloat[0, colour, rows], vfloat[1, colour, rows]
                for mom in range(4):
                    cosine, sine = cosines[mom, at, :], sines[mom, at, :]
                    pr = (cosine * vr + sine * vi).astype(jnp.bfloat16)
                    pi = (cosine * vi - sine * vr).astype(jnp.bfloat16)
                    upper, lower = pl.ds(mom * 128 + odd * 32, 32), pl.ds(mom * 128 + 64 + odd * 32, 32)
                    first, second = pl.ds(colour * 128, 128), pl.ds((3 + colour) * 128, 128)
                    right[upper, first] = pr
                    right[upper, second] = -pi
                    right[lower, first] = pi
                    right[lower, second] = pr
        product = lax.dot_general(
            left[...], right[...], (((1,), (1,)), ((), ())), preferred_element_type=jnp.float32
        )
        for mom in range(4):
            total[mom] += product[:, mom * 128 : (mom + 1) * 128]

    def body(n, carry):
        rel = jnp.where(n % 2 == 1, NZ - (n + 1) // 2, n // 2)
        contract(0, rel)

        @pl.when(n == 0)
        def _():
            relay(1)

        @pl.when(n < 6)
        def _():
            relay(n + 2)

        for colour in range(3):
            pair_copy(rel, colour).wait_recv()
        contract(1, rel)
        return carry

    lax.fori_loop(0, NZ, body, 0)

    def sum_copy(group, step):
        return pltpu.make_async_remote_copy(
            src_ref=outbox.at[step - 1, group],
            dst_ref=inbox.at[step - 1, group],
            send_sem=sum_send.at[group, step - 1],
            recv_sem=sum_recv.at[group, step - 1],
            device_id=across[step - 1],
            device_id_type=MESH,
        )

    def share_copy(group, step):
        return pltpu.make_async_remote_copy(
            src_ref=chunk.at[group],
            dst_ref=all_chunks.at[group, slot_q],
            send_sem=share_send.at[group, step - 1],
            recv_sem=share_recv.at[group, step - 1],
            device_id=along[step - 1],
            device_id_type=MESH,
        )

    def share_arrival(group, step):
        return pltpu.make_async_remote_copy(
            src_ref=chunk.at[group],
            dst_ref=all_chunks.at[group, (zz + HALF - step) % HALF * NC + c],
            send_sem=share_send.at[group, step - 1],
            recv_sem=share_recv.at[group, step - 1],
            device_id=along[step - 1],
            device_id_type=MESH,
        )

    def swap_copy(group, step, core):
        slot = (zz + HALF - step) % HALF * NC + core
        return pltpu.make_async_remote_copy(
            src_ref=chunk.at[group] if step == 0 else all_chunks.at[group, slot],
            dst_ref=all_chunks.at[group, slot],
            send_sem=swap_send.at[group, step],
            recv_sem=swap_recv.at[group, step],
            device_id=partner,
            device_id_type=MESH,
        )

    for group in range(4):
        where = pl.ds(group * 64, 64)
        for step in (2, 1, 3):
            outbox[step - 1, group] = total[(x + step) % NX, where].astype(jnp.bfloat16)
            sum_copy(group, step).start()

    per_local.wait()
    for step, copy in enumerate(per_copies, 1):
        copy.wait_send()
        pltpu.make_async_remote_copy(
            src_ref=per_ref.at[y],
            dst_ref=arrived.at[(y + NY - step) % NY],
            send_sem=per_send.at[step - 1],
            recv_sem=per_recv.at[step - 1],
            device_id=sinks[step - 1],
            device_id_type=MESH,
        ).wait_recv()

    low = lax.broadcasted_iota(jnp.int32, (32, 128), 1) < 64
    even = lax.broadcasted_iota(jnp.int32, (32, 128), 1) % 2 == 0
    row = lax.broadcasted_iota(jnp.int32, (16, 128), 0)
    lane = lax.broadcasted_iota(jnp.int32, (16, 128), 1)
    rank = lax.axis_index("space") % 8
    pick = (lane == (row // 8) * 64 + rank * 8 + row % 8).astype(jnp.float32).astype(jnp.bfloat16)
    row = lax.broadcasted_iota(jnp.int32, (128, 128), 0)
    lane = lax.broadcasted_iota(jnp.int32, (128, 128), 1)
    wanted = (row % 2) * 64 + 2 * (row % 64 // 2) + row // 64
    order = (lane == wanted).astype(jnp.float32).astype(jnp.bfloat16)

    def rolled(value):
        return pltpu.roll(value, 64, 1)

    def tau(which, quark):
        source, comb = sources_ref[which // 2], which % 2
        spin = spins_ref[comb, 0, quark] * 4 + spins_ref[comb, 1, quark]
        flat = arrived[source, spin].astype(jnp.float32)
        for pair in range(32):
            wide[quark, 2 * pair : 2 * pair + 2, :] = flat[:, pair * 128 : (pair + 1) * 128]
        return wide[quark, pl.ds(0, 32, stride=2), :], wide[quark, pl.ds(1, 32, stride=2), :]

    def both_of_pair(value):
        turned, zero = rolled(value), jnp.zeros_like(value)
        return jnp.concatenate(
            [
                jnp.where(low, value, zero),
                jnp.where(low, turned, zero),
                jnp.where(low, zero, turned),
                jnp.where(low, zero, value),
            ],
            axis=0,
        ).astype(jnp.bfloat16)

    def arranged(upper, lower):
        uturn, lturn = rolled(upper), rolled(lower)
        straight = jnp.where(low, jnp.where(even, upper, uturn), jnp.where(even, lturn, lower))
        turned = jnp.where(low, jnp.where(even, uturn, upper), jnp.where(even, lower, lturn))
        return [straight, turned]

    def operators(which, carry):
        real, imag = tau(which, 0)
        upper = jnp.concatenate([real, rolled(real), -imag, -rolled(imag)], axis=0)
        lower = jnp.concatenate([rolled(imag), imag, rolled(real), real], axis=0)
        lanes = lax.broadcasted_iota(jnp.int32, (128, 128), 1)
        picked = lax.dot_general(
            pick,
            jnp.where(lanes < 64, upper, lower).astype(jnp.bfloat16),
            (((1,), (1,)), ((), ())),
            preferred_element_type=jnp.float32,
        )
        for part in range(2):
            at = pl.ds(pl.multiple_of(part * 64 + which * 8, 8), 8)
            first_op[at, :] = picked[part * 8 : part * 8 + 8]
        real, imag = tau(which, 2)
        second_op_ref[which, 0] = both_of_pair(real)
        second_op_ref[which, 1] = both_of_pair(imag)
        real, imag = tau(which, 1)
        operator = jnp.concatenate(arranged(real, imag) + arranged(-imag, real), axis=0)
        third_op_ref[which] = lax.dot_general(
            order, operator.astype(jnp.bfloat16), (((1,), (1,)), ((), ())),
            preferred_element_type=jnp.float32,
        ).astype(jnp.bfloat16)
        return carry

    lax.fori_loop(0, 4, operators, 0)

    for group in range(4):
        where = pl.ds(group * 64, 64)
        for step in (1, 2, 3):
            sum_copy(group, step).wait_recv()
        summed = total[x, where]
        for step in range(3):
            summed = summed + inbox[step, group].astype(jnp.float32)
        chunk[group] = summed.astype(jnp.bfloat16)
        for step in (3, 2, 1):
            share_copy(group, step).start()
        swap_copy(group, 0, c).start()
        all_chunks[group, slot_q] = chunk[group]

    lax.fori_loop(4, 8, operators, 0)
    full[pl.ds(0, 32, stride=129), :] = jnp.zeros((32, 128), jnp.float32)
    full[pl.ds(96, 32, stride=129), :] = jnp.zeros((32, 128), jnp.float32)

    def onward(group):
        for step in (1, 3, 2):
            share_arrival(group, step).wait_recv()
            swap_copy(group, step, c).start()

    def expand(group):
        for step in range(HALF):
            swap_copy(group, step, 1 - c).wait_recv()
        for q in range(8):
            d = 1 + q + 8 * group
            for odd in range(2):
                piece = all_chunks[group, q, odd * 32 : odd * 32 + 32, :].astype(jnp.float32)
                kodd = (odd + d) % 2
                e = (odd + d - kodd) // 2
                base = odd * 64 + kodd * 32 + e
                full[pl.ds(base, 32 - e, stride=129), :] = piece[: 32 - e]
                if e:
                    full[pl.ds(129 * (32 - e) + base - 32, e, stride=129), :] = piece[32 - e :]
                if d < 32:
                    base = 128 * e + kodd * 64 + odd * 32
                    full[pl.ds(base, 32 - e, stride=129), :] = -piece[: 32 - e]
                    if e:
                        full[pl.ds(129 * (32 - e) + base - 4096, e, stride=129), :] = -piece[32 - e :]

    onward(0)
    onward(1)
    expand(0)
    onward(2)
    expand(1)
    onward(3)
    expand(2)
    expand(3)

    operator = first_op[...].astype(jnp.bfloat16)
    for two in range(16):
        block = full[two * 256 : (two + 1) * 256, :].astype(jnp.bfloat16)
        first = lax.dot_general(
            operator, block, (((1,), (1,)), ((), ())), preferred_element_type=jnp.float32
        )
        for part in range(2):
            for which in range(8):
                at = part * 64 + which * 8
                piece = jnp.concatenate([first[at : at + 8, :128], first[at : at + 8, 128:]], axis=0)
                rows_ref[which, two * 16 : two * 16 + 16, part * 128 : (part + 1) * 128] = piece.astype(jnp.bfloat16)

    for rel in range(NZ):
        for colour in range(3):
            if rel in (7, 6, 5, 4):
                ring_copy((rel + 1) % NZ, colour, True).wait_send()
            elif rel:
                ring_copy(rel - 1, colour, False).wait_send()
            pair_copy(rel, colour).wait_send()
    for group in range(4):
        for step in (1, 2, 3):
            sum_copy(group, step).wait_send()
            share_copy(group, step).wait_send()
        for step in range(HALF):
            swap_copy(group, step, c).wait_send()


def first_contraction(vecs, momenta, sources, spins, perams):
    vmem = pl.BlockSpec(memory_space=pltpu.VMEM)
    smem = pl.BlockSpec(memory_space=pltpu.SMEM)
    dma, bf16, f32 = pltpu.SemaphoreType.DMA, jnp.bfloat16, jnp.float32
    return pl.pallas_call(
        elemental_kernel,
        out_shape=(
            jax.ShapeDtypeStruct((8, 256, 256), bf16),
            jax.ShapeDtypeStruct((8, 2, 128, 128), bf16),
            jax.ShapeDtypeStruct((8, 128, 128), bf16),
        ),
        in_specs=[vmem, smem, smem, smem, pl.BlockSpec(memory_space=pl.ANY)],
        out_specs=(vmem, vmem, vmem),
        scratch_shapes=[
            pltpu.VMEM((4, NC * NZ, 128), f32),
            pltpu.VMEM((4, NC * NZ, 128), f32),
            pltpu.VMEM((NC, NZ, 2, 3, 64, 128), bf16),
            pltpu.VMEM((2, 3, 128, 128), f32),
            pltpu.VMEM((256, 768), bf16),
            pltpu.VMEM((512, 768), bf16),
            pltpu.VMEM((4, 256, 128), f32),
            pltpu.VMEM((3, 4, 64, 128), bf16),
            pltpu.VMEM((3, 4, 64, 128), bf16),
            pltpu.VMEM((4, 64, 128), bf16),
            pltpu.VMEM((4, 8, 64, 128), bf16),
            pltpu.VMEM(perams.shape, bf16),
            pltpu.VMEM((3, 64, 128), f32),
            pltpu.VMEM((4096, 128), f32),
            pltpu.VMEM((128, 128), f32),
            dma((NZ, 3)), dma((NZ, 3)), dma((NZ, 3)), dma((NZ, 3)),
            dma((4, 3)), dma((4, 3)), dma((4, 3)), dma((4, 3)), dma((4, 4)), dma((4, 4)),
            dma((3,)), dma((3,)), dma(()), dma(()),
        ],
        compiler_params=pltpu.CompilerParams(collective_id=0, has_side_effects=True),
    )(vecs, momenta, sources, spins, perams)


def contract_kernel(rows_ref, second_op_ref, third_op_ref, out_ref, second):
    kreal, kimag = second_op_ref[0, 0], second_op_ref[0, 1]
    operator = jnp.concatenate(
        [jnp.concatenate([kreal, kimag], axis=1), jnp.concatenate([-kimag, kreal], axis=1)], axis=0
    )
    product = jnp.dot(rows_ref[0], operator, preferred_element_type=jnp.float32)
    for part in range(2):
        second[part] = product[:, part * 128 : (part + 1) * 128]
    keep = lax.broadcasted_iota(jnp.int32, (64, 128), 1) < 64
    for i in range(8):
        parts = []
        for part in range(2):
            straight = second[part, pl.ds(i, 32, stride=8), :]
            parts += [straight, pltpu.roll(straight, 64, 1)]
        operand = jnp.concatenate(parts, axis=0).astype(jnp.bfloat16)
        both = jnp.dot(third_op_ref[0], operand, preferred_element_type=jnp.float32)
        out_ref[i] = jnp.where(keep, both[:64], both[64:])


def last_contractions(rows, second_op, third_op):
    return pl.pallas_call(
        contract_kernel,
        grid=(8,),
        out_shape=jax.ShapeDtypeStruct((64, 64, 128), jnp.float32),
        in_specs=[
            pl.BlockSpec((1, 256, 256), lambda s: (s, 0, 0)),
            pl.BlockSpec((1, 2, 128, 128), lambda s: (s, 0, 0, 0)),
            pl.BlockSpec((1, 128, 128), lambda s: (s, 0, 0)),
        ],
        out_specs=pl.BlockSpec((8, 64, 128), lambda s: (s, 0, 0)),
        scratch_shapes=[pltpu.VMEM((2, 256, 128), jnp.float32)],
        compiler_params=pltpu.CompilerParams(dimension_semantics=("arbitrary",)),
    )(rows, second_op, third_op)


def on_device(eigvecs, momenta, perams, sources, spins):
    operands = first_contraction(
        eigvecs[0], jnp.transpose(momenta), sources, jnp.transpose(spins, (0, 2, 1)), perams[0]
    )
    result = last_contractions(*operands)
    result = jnp.transpose(result.reshape(64, 32, 2, 128), (0, 2, 1, 3))
    return result.reshape(1, 4, 2, 8, 2, 4096)


def solution(mesh):
    placed = (
        P("tpair", None, None, None, "space"),
        P(),
        P("tpair", None, None, None, None),
        P(),
        P(),
    )
    return jax.shard_map(
        on_device,
        mesh=mesh,
        in_specs=placed,
        out_specs=P("tpair", None, None, "space", None, None),
        check_vma=False,
    )
```

time: 55.2 us -> 50 us (0.906)
  local copies, waits for them, and re-layouts: 2.71 us -> 0 us
  Pallas kernels: 52.2 us -> 49.7 us
    unnamed x2 -> x0, local copies, waits for them, and re-layouts: 2.71 us -> none
    pallas_call x2, Pallas kernels: 52.2 us -> 49.7 us  [the longest x1 42.1 us: first_contraction(): pl.pallas_call(elemental_kernel, out_shape=(jax.ShapeDtypeStruct((8, 256,...]
where the time goes in v2:
time: 50 us; the launch traced here: 49.8 us
  Pallas kernels  49.7 us (99%)
    pallas_call x1, Pallas kernels, first_contraction(): pl.pallas_call(elemental_kernel, out_shape=(jax.ShapeDtypeStruct((8, 256,...  42.1 us
    pallas_call x1, Pallas kernels, last_contractions(): pl.pallas_call(contract_kernel, grid=(8,), out_shape=jax.ShapeDtypeStruct...  7.65 us

profile of v2, /device:TPU:1, one launch (start us, length us, event | category | flops | bytes accessed | tf_op | source)
XLA Modules:
  0.0 49.8 jit_solution(9084619470871904225)
XLA Ops:
  0.0 42.1 %shard_map.55 = (bf16[8,256,256]{2,1,0:T(8,128)(2,1)}, bf16[8,2,128,128]{3,2,1,0:T(8,128)(2,1)}, bf16[8,128,128]{2,1,0:T(8,128)(2,1)}) custom-call(bf16[2,3,64,128]{3,2,1,0:T(8,128)(2,1)} %bitcast.10, s32[3,8]{1,0:T(4,128)} %bitcast.11, s32[4]{0:T(128)} %sources_ref.1, s32[2,2,3]{2,1,0:T(2,128)} %bitcast.12, bf16[4,16,2,4096]{3,2,1,0:T(2,128)(2,1)} %bitcast.9), custom_call_target="tpu_custom_call" | custom-call | tf_op jit(solution)/shard_map/pallas_call | solution.py:402
  42.1 7.6 %shard_map.56 = f32[64,64,128]{2,1,0:T(8,128)} custom-call(bf16[8,256,256]{2,1,0:T(8,128)(2,1)} %get-tuple-element.8.rows_ref, bf16[8,2,128,128]{3,2,1,0:T(8,128)(2,1)} %get-tuple-element.9.second_op_ref, bf16[8,128,128]{2,1,0:T(8,128)(2,1)} %get-tuple-element.10.third_op_ref), custom_call_target="tpu_custom_call" | custom-call | tf_op jit(solution)/shard_map/pallas_call | solution.py:455

commit v3 on v2

v3 whole, which is shorter than its diff:
```python
import functools

import jax
import jax.numpy as jnp
from jax import lax
from jax.experimental import pallas as pl
from jax.experimental.pallas import tpu as pltpu
from jax.sharding import PartitionSpec as P

LEXT = 64
TWO_PI = 6.283185307179586
MESH = pl.DeviceIdType.MESH

NX, NZ, NC = 4, 8, 2
NY = 4
HALF = NZ // 2
PER_STEP = 2


def place():
    index = lax.axis_index("space")
    return lax.div(index, NZ * NC), lax.rem(lax.div(index, NC), NZ), lax.rem(index, NC)


def at_space(x, z, c):
    return {"space": (x * NZ + z) * NC + c}


def elemental_kernel(
    vec_ref, mom_hbm, sources_hbm, spins_hbm, per_ref, rows_ref, second_op_ref, third_op_ref,
    cosines, sines, fields, vfloat, left, right, total, core_in, own_sum, outbox, inbox, chunk, all_chunks,
    arrived, wide, full, first_op, mom_ref, sources_ref, spins_ref, small_sem, own_sem, ring_send, ring_recv, core_send, core_recv, sum_send, sum_recv,
    share_send, share_recv, swap_send, swap_recv, per_send, per_recv, per_own,
):
    x, z, c = place()
    y = lax.axis_index("tpair")
    zhalf, zz = lax.div(z, HALF), lax.rem(z, HALF)
    slot_q = zz * NC + c
    on_right = at_space(x, lax.rem(z + 1, NZ), c)
    on_left = at_space(x, lax.rem(z + NZ - 1, NZ), c)
    partner = at_space(x, z, 1 - c)
    across = [at_space(lax.rem(x + step, NX), z, c) for step in range(1, NX)]
    along = [at_space(x, zhalf * HALF + lax.rem(zz + step, HALF), c) for step in range(1, HALF)]
    sinks = [{"tpair": lax.rem(y + step, NY)} for step in range(1, NY)]

    barrier = pltpu.get_barrier_semaphore()
    greeted = [on_right, on_left, partner] + across + along + sinks
    for target in greeted:
        pl.semaphore_signal(barrier, inc=1, device_id=target, device_id_type=MESH)
    own = pltpu.make_async_copy(vec_ref, fields.at[0], own_sem)
    own.start()
    small = [
        pltpu.make_async_copy(mom_hbm, mom_ref, small_sem.at[0]),
        pltpu.make_async_copy(sources_hbm, sources_ref, small_sem.at[1]),
        pltpu.make_async_copy(spins_hbm, spins_ref, small_sem.at[2]),
    ]
    for copy in small:
        copy.start()
    pl.semaphore_wait(barrier, len(greeted))
    own.wait()

    def remote(source, target, send_sem, recv_sem, device):
        return pltpu.make_async_remote_copy(
            src_ref=source, dst_ref=target, send_sem=send_sem, recv_sem=recv_sem,
            device_id=device, device_id_type=MESH,
        )

    def ring_copy(rel, part, rightward):
        there = (rel + NZ - 1) % NZ if rightward else (rel + 1) % NZ
        return remote(
            fields.at[rel, part], fields.at[there, part], ring_send, ring_recv.at[there, part],
            on_right if rightward else on_left,
        )

    for part in range(2):
        ring_copy(0, part, True).start()
        ring_copy(0, part, False).start()

    for step in range(1, NY):
        remote(per_ref.at[lax.rem(y + step, NY)], arrived.at[y], per_send, per_recv, sinks[step - 1]).start()
    per_local = pltpu.make_async_copy(per_ref.at[y], arrived.at[y], per_own)
    per_local.start()

    def relay(step):
        for part in range(2):
            if step < HALF or part == 0:
                rel = NZ - step
                remote(fields.at[rel, part], fields.at[rel, part], ring_send, ring_recv.at[rel, part], on_right).wait_recv()
                if step < HALF - 1 or (step == HALF - 1 and part == 0):
                    ring_copy(rel, part, True).start()
            if step < HALF or part == 1:
                rel = step
                remote(fields.at[rel, part], fields.at[rel, part], ring_send, ring_recv.at[rel, part], on_left).wait_recv()
                if step < HALF - 1 or (step == HALF - 1 and part == 1):
                    ring_copy(rel, part, False).start()

    for copy in small:
        copy.wait()

    row = lax.broadcasted_iota(jnp.int32, (NZ, 128), 0)
    lane = lax.broadcasted_iota(jnp.int32, (NZ, 128), 1)
    sites = ((x * NZ + ((z + row) & (NZ - 1))) * NC + c) * 128 + lane
    xs, ys, zs = sites & (LEXT - 1), (sites >> 6) & (LEXT - 1), sites >> 12
    factor = lax.rsqrt(jnp.float32(24.0 * 128 * NX * NZ * NC))
    for mom in range(4):
        mine = 2 * mom + zhalf
        turns = mom_ref[0, mine] * xs + mom_ref[1, mine] * ys + mom_ref[2, mine] * zs
        angle = (turns & (LEXT - 1)).astype(jnp.float32) * (TWO_PI / LEXT)
        cosines[mom] = jnp.cos(angle) * factor
        sines[mom] = jnp.sin(angle) * factor

    total[...] = jnp.zeros_like(total)

    def contract(rel):
        for part in range(2):
            for colour in range(3):
                values = fields[rel, part, colour].astype(jnp.float32)
                vfloat[part, colour, 0:64] = values
                vfloat[part, colour, 64:128] = values
        for colour in range(3):
            nxt, aft = (colour + 1) % 3, (colour + 2) % 3
            for odd in range(2):
                rows = pl.ds(odd, 32, stride=2)
                lrn, lin = vfloat[0, nxt, rows], vfloat[1, nxt, rows]
                lra, lia = vfloat[0, aft, rows], vfloat[1, aft, rows]
                for core in range(2):
                    for group in range(4):
                        rows = pl.ds(1 + zz * NC + core + 8 * group + odd, 32, stride=2)
                        rrn, rin = vfloat[0, nxt, rows], vfloat[1, nxt, rows]
                        rra, ria = vfloat[0, aft, rows], vfloat[1, aft, rows]
                        real = lrn * rra - lin * ria - (lra * rrn - lia * rin)
                        imag = lrn * ria + lin * rra - (lra * rin + lia * rrn)
                        where = pl.ds(core * 256 + group * 64 + odd * 32, 32)
                        left[where, colour * 128 : (colour + 1) * 128] = real.astype(jnp.bfloat16)
                        left[where, (3 + colour) * 128 : (4 + colour) * 128] = imag.astype(jnp.bfloat16)
        at = pl.ds(rel, 1)
        for colour in range(3):
            for odd in range(2):
                rows = pl.ds(odd, 32, stride=2)
                vr, vi = vfloat[0, colour, rows], vfloat[1, colour, rows]
                for mom in range(4):
                    cosine, sine = cosines[mom, at, :], sines[mom, at, :]
                    pr = (cosine * vr + sine * vi).astype(jnp.bfloat16)
                    pi = (cosine * vi - sine * vr).astype(jnp.bfloat16)
                    upper, lower = pl.ds(mom * 128 + odd * 32, 32), pl.ds(mom * 128 + 64 + odd * 32, 32)
                    first, second = pl.ds(colour * 128, 128), pl.ds((3 + colour) * 128, 128)
                    right[upper, first] = pr
                    right[upper, second] = -pi
                    right[lower, first] = pi
                    right[lower, second] = pr
        product = lax.dot_general(
            left[...], right[...], (((1,), (1,)), ((), ())), preferred_element_type=jnp.float32
        )
        for core in range(2):
            for group in range(4):
                at = core * 256 + group * 64
                for mom in range(4):
                    total[core, group, mom] += product[at : at + 64, mom * 128 : (mom + 1) * 128]

    def body(n, carry):
        contract(jnp.where(n % 2 == 1, NZ - (n + 1) // 2, n // 2))
        for after, step in ((0, 1), (1, 2), (3, 3), (5, 4)):
            pl.when(n == after)(functools.partial(relay, step))
        return carry

    lax.fori_loop(0, NZ, body, 0)

    for group in range(4):
        remote(total.at[1 - c, group], core_in.at[group], core_send, core_recv.at[group], partner).start()

    def share_arrival(group, step):
        owner = lax.rem(zz + HALF - step, HALF) * NC + c
        return remote(
            chunk.at[group], all_chunks.at[group, owner], share_send, share_recv.at[group, step - 1], along[step - 1]
        )

    def swap_copy(group, step):
        owner = lax.rem(zz + HALF - step, HALF) * NC + c
        return remote(
            chunk.at[group] if step == 0 else all_chunks.at[group, owner],
            all_chunks.at[group, owner], swap_send, swap_recv.at[group], partner,
        )

    per_local.wait()
    remote(per_ref.at[0:3], arrived.at[0:3], per_send, per_recv, sinks[0]).wait()

    low = lax.broadcasted_iota(jnp.int32, (32, 128), 1) < 64
    even = lax.broadcasted_iota(jnp.int32, (32, 128), 1) % 2 == 0
    row = lax.broadcasted_iota(jnp.int32, (16, 128), 0)
    lane = lax.broadcasted_iota(jnp.int32, (16, 128), 1)
    rank = lax.axis_index("space") % 8
    pick = (lane == (row // 8) * 64 + rank * 8 + row % 8).astype(jnp.float32).astype(jnp.bfloat16)
    row = lax.broadcasted_iota(jnp.int32, (128, 128), 0)
    lane = lax.broadcasted_iota(jnp.int32, (128, 128), 1)
    wanted = (row % 2) * 64 + 2 * (row % 64 // 2) + row // 64
    order = (lane == wanted).astype(jnp.float32).astype(jnp.bfloat16)

    def rolled(value):
        return pltpu.roll(value, 64, 1)

    def tau(which, quark):
        source, comb = sources_ref[which // 2], which % 2
        spin = spins_ref[comb, 0, quark] * 4 + spins_ref[comb, 1, quark]
        flat = arrived[source, spin].astype(jnp.float32)
        for pair in range(32):
            wide[quark, 2 * pair : 2 * pair + 2, :] = flat[:, pair * 128 : (pair + 1) * 128]
        return wide[quark, pl.ds(0, 32, stride=2), :], wide[quark, pl.ds(1, 32, stride=2), :]

    def both_of_pair(value):
        turned, zero = rolled(value), jnp.zeros_like(value)
        return jnp.concatenate(
            [
                jnp.where(low, value, zero),
                jnp.where(low, turned, zero),
                jnp.where(low, zero, turned),
                jnp.where(low, zero, value),
            ],
            axis=0,
        ).astype(jnp.bfloat16)

    def arranged(upper, lower):
        uturn, lturn = rolled(upper), rolled(lower)
        straight = jnp.where(low, jnp.where(even, upper, uturn), jnp.where(even, lturn, lower))
        turned = jnp.where(low, jnp.where(even, uturn, upper), jnp.where(even, lower, lturn))
        return [straight, turned]

    def operators(which, carry):
        real, imag = tau(which, 0)
        upper = jnp.concatenate([real, rolled(real), -imag, -rolled(imag)], axis=0)
        lower = jnp.concatenate([rolled(imag), imag, rolled(real), real], axis=0)
        lanes = lax.broadcasted_iota(jnp.int32, (128, 128), 1)
        picked = lax.dot_general(
            pick,
            jnp.where(lanes < 64, upper, lower).astype(jnp.bfloat16),
            (((1,), (1,)), ((), ())),
            preferred_element_type=jnp.float32,
        )
        for part in range(2):
            at = pl.ds(pl.multiple_of(part * 64 + which * 8, 8), 8)
            first_op[at, :] = picked[part * 8 : part * 8 + 8]
        real, imag = tau(which, 2)
        second_op_ref[which, 0] = both_of_pair(real)
        second_op_ref[which, 1] = both_of_pair(imag)
        real, imag = tau(which, 1)
        operator = jnp.concatenate(arranged(real, imag) + arranged(-imag, real), axis=0)
        third_op_ref[which] = lax.dot_general(
            order, operator.astype(jnp.bfloat16), (((1,), (1,)), ((), ())),
            preferred_element_type=jnp.float32,
        ).astype(jnp.bfloat16)
        return carry

    lax.fori_loop(0, 2, operators, 0)

    for group in range(4):
        remote(core_in.at[group], core_in.at[group], core_send, core_recv.at[group], partner).wait_recv()
        for step in (2, 1, 3):
            mom = lax.rem(x + step, NX)
            outbox[group, step - 1] = (total[c, group, mom] + core_in[group, mom]).astype(jnp.bfloat16)
            remote(
                outbox.at[group, step - 1], inbox.at[group, step - 1], sum_send, sum_recv.at[group], across[step - 1]
            ).start()
        own_sum[group] = total[c, group, x] + core_in[group, x]

    lax.fori_loop(2, 5, operators, 0)

    for group in range(4):
        remote(inbox.at[group], inbox.at[group], sum_send, sum_recv.at[group], across[0]).wait_recv()
        summed = own_sum[group]
        for step in range(3):
            summed = summed + inbox[group, step].astype(jnp.float32)
        chunk[group] = summed.astype(jnp.bfloat16)
        for step in (3, 2, 1):
            remote(
                chunk.at[group], all_chunks.at[group, slot_q], share_send, share_recv.at[group, step - 1], along[step - 1]
            ).start()
        swap_copy(group, 0).start()
        all_chunks[group, slot_q] = chunk[group]

    lax.fori_loop(5, 8, operators, 0)
    full[pl.ds(0, 32, stride=129), :] = jnp.zeros((32, 128), jnp.float32)
    full[pl.ds(96, 32, stride=129), :] = jnp.zeros((32, 128), jnp.float32)

    def onward(group):
        for step in (1, 3, 2):
            share_arrival(group, step).wait_recv()
            swap_copy(group, step).start()

    def expand(group):
        remote(chunk, chunk, swap_send, swap_recv.at[group], partner).wait_recv()
        for q in range(8):
            d = 1 + q + 8 * group
            for odd in range(2):
                piece = all_chunks[group, q, odd * 32 : odd * 32 + 32, :].astype(jnp.float32)
                kodd = (odd + d) % 2
                e = (odd + d - kodd) // 2
                base = odd * 64 + kodd * 32 + e
                full[pl.ds(base, 32 - e, stride=129), :] = piece[: 32 - e]
                if e:
                    full[pl.ds(129 * (32 - e) + base - 32, e, stride=129), :] = piece[32 - e :]
                if d < 32:
                    base = 128 * e + kodd * 64 + odd * 32
                    full[pl.ds(base, 32 - e, stride=129), :] = -piece[: 32 - e]
                    if e:
                        full[pl.ds(129 * (32 - e) + base - 4096, e, stride=129), :] = -piece[32 - e :]

    onward(0)
    onward(1)
    expand(0)
    onward(2)
    expand(1)
    onward(3)
    expand(2)
    expand(3)

    operator = first_op[...].astype(jnp.bfloat16)
    for two in range(16):
        block = full[two * 256 : (two + 1) * 256, :].astype(jnp.bfloat16)
        first = lax.dot_general(
            operator, block, (((1,), (1,)), ((), ())), preferred_element_type=jnp.float32
        )
        for part in range(2):
            for which in range(8):
                at = part * 64 + which * 8
                piece = jnp.concatenate([first[at : at + 8, :128], first[at : at + 8, 128:]], axis=0)
                rows_ref[which, two * 16 : two * 16 + 16, part * 128 : (part + 1) * 128] = piece.astype(jnp.bfloat16)

    remote(fields.at[0:7], fields.at[0:7], ring_send, ring_recv.at[0, 0], on_right).wait_send()
    remote(core_in, core_in, core_send, core_recv.at[0], partner).wait_send()
    remote(outbox, inbox, sum_send, sum_recv.at[0], across[0]).wait_send()
    remote(outbox, inbox, share_send, share_recv.at[0, 0], along[0]).wait_send()
    remote(all_chunks.at[0:2], all_chunks.at[0:2], swap_send, swap_recv.at[0], partner).wait_send()


def first_contraction(vecs, momenta, sources, spins, perams):
    vmem = pl.BlockSpec(memory_space=pltpu.VMEM)
    hbm = pl.BlockSpec(memory_space=pltpu.HBM)
    dma, bf16, f32 = pltpu.SemaphoreType.DMA, jnp.bfloat16, jnp.float32
    return pl.pallas_call(
        elemental_kernel,
        out_shape=(
            jax.ShapeDtypeStruct((8, 256, 256), bf16),
            jax.ShapeDtypeStruct((8, 2, 128, 128), bf16),
            jax.ShapeDtypeStruct((8, 128, 128), bf16),
        ),
        in_specs=[hbm, hbm, hbm, hbm, hbm],
        out_specs=(vmem, vmem, vmem),
        scratch_shapes=[
            pltpu.VMEM((4, NZ, 128), f32),
            pltpu.VMEM((4, NZ, 128), f32),
            pltpu.VMEM((NZ, 2, 3, 64, 128), bf16),
            pltpu.VMEM((2, 3, 128, 128), f32),
            pltpu.VMEM((512, 768), bf16),
            pltpu.VMEM((512, 768), bf16),
            pltpu.VMEM((2, 4, 4, 64, 128), f32),
            pltpu.VMEM((4, 4, 64, 128), f32),
            pltpu.VMEM((4, 64, 128), f32),
            pltpu.VMEM((4, 3, 64, 128), bf16),
            pltpu.VMEM((4, 3, 64, 128), bf16),
            pltpu.VMEM((4, 64, 128), bf16),
            pltpu.VMEM((4, 8, 64, 128), bf16),
            pltpu.VMEM(perams.shape, bf16),
            pltpu.VMEM((3, 64, 128), f32),
            pltpu.VMEM((4096, 128), f32),
            pltpu.VMEM((128, 128), f32),
            pltpu.SMEM((3, 8), jnp.int32),
            pltpu.SMEM((4,), jnp.int32),
            pltpu.SMEM((2, 2, 3), jnp.int32),
            dma((3,)), dma(()), dma(()), dma((NZ, 2)), dma(()), dma((4,)), dma(()), dma((4,)),
            dma(()), dma((4, 3)), dma(()), dma((4,)), dma(()), dma(()), dma(()),
        ],
        compiler_params=pltpu.CompilerParams(
            collective_id=0, has_side_effects=True, vmem_limit_bytes=20 << 20
        ),
    )(*[pltpu.with_memory_space_constraint(value, pltpu.HBM) for value in (vecs, momenta, sources, spins, perams)])


def contract_kernel(rows_ref, second_op_ref, third_op_ref, out_ref, second):
    keep = lax.broadcasted_iota(jnp.int32, (64, 128), 1) < 64
    for which in range(PER_STEP):
        kreal, kimag = second_op_ref[which, 0], second_op_ref[which, 1]
        operator = jnp.concatenate(
            [jnp.concatenate([kreal, kimag], axis=1), jnp.concatenate([-kimag, kreal], axis=1)], axis=0
        )
        product = jnp.dot(rows_ref[which], operator, preferred_element_type=jnp.float32)
        for part in range(2):
            second[which, part] = product[:, part * 128 : (part + 1) * 128]
    for which in range(PER_STEP):
        columns = []
        for i in range(8):
            parts = []
            for part in range(2):
                straight = second[which, part, pl.ds(i, 32, stride=8), :]
                parts += [straight, pltpu.roll(straight, 64, 1)]
            columns.append(jnp.concatenate(parts, axis=0).astype(jnp.bfloat16))
        both = jnp.dot(third_op_ref[which], jnp.concatenate(columns, axis=1), preferred_element_type=jnp.float32)
        for i in range(8):
            lanes = slice(i * 128, (i + 1) * 128)
            out_ref[which * 8 + i] = jnp.where(keep, both[:64, lanes], both[64:, lanes])


def last_contractions(rows, second_op, third_op):
    return pl.pallas_call(
        contract_kernel,
        grid=(8 // PER_STEP,),
        out_shape=jax.ShapeDtypeStruct((64, 64, 128), jnp.float32),
        in_specs=[
            pl.BlockSpec((PER_STEP, 256, 256), lambda s: (s, 0, 0)),
            pl.BlockSpec((PER_STEP, 2, 128, 128), lambda s: (s, 0, 0, 0)),
            pl.BlockSpec((PER_STEP, 128, 128), lambda s: (s, 0, 0)),
        ],
        out_specs=pl.BlockSpec((8 * PER_STEP, 64, 128), lambda s: (s, 0, 0)),
        scratch_shapes=[pltpu.VMEM((PER_STEP, 2, 256, 128), jnp.float32)],
        compiler_params=pltpu.CompilerParams(
            dimension_semantics=("arbitrary",), vmem_limit_bytes=16 << 20
        ),
    )(rows, second_op, third_op)


def on_device(eigvecs, momenta, perams, sources, spins):
    operands = first_contraction(
        eigvecs[0], jnp.transpose(momenta), sources, jnp.transpose(spins, (0, 2, 1)), perams[0]
    )
    result = last_contractions(*operands)
    result = jnp.transpose(result.reshape(64, 32, 2, 128), (0, 2, 1, 3))
    return result.reshape(1, 4, 2, 8, 2, 4096)


def solution(mesh):
    placed = (
        P("tpair", None, None, None, "space"),
        P(),
        P("tpair", None, None, None, None),
        P(),
        P(),
    )
    return jax.shard_map(
        on_device,
        mesh=mesh,
        in_specs=placed,
        out_specs=P("tpair", None, None, "space", None, None),
        check_vma=False,
    )
```

time: 50 us -> 45 us (0.900)
  Pallas kernels: 49.7 us -> 44.9 us
    pallas_call x1, Pallas kernels: 7.65 us -> 3.48 us  [last_contractions(): pl.pallas_call(contract_kernel, grid=(8 // PER_STEP,), out_shape=jax.Shap...]
    pallas_call x1, Pallas kernels: 42.1 us -> 41.4 us  [first_contraction(): pl.pallas_call(elemental_kernel, out_shape=(jax.ShapeDtypeStruct((8, 256,...]
where the time goes in v3:
time: 45 us; the launch traced here: 44.9 us
  Pallas kernels  44.9 us (100%)
    pallas_call x1, Pallas kernels, first_contraction(): pl.pallas_call(elemental_kernel, out_shape=(jax.ShapeDtypeStruct((8, 256,...  41.4 us
    pallas_call x1, Pallas kernels, last_contractions(): pl.pallas_call(contract_kernel, grid=(8 // PER_STEP,), out_shape=jax.Shap...  3.48 us

profile of v3, /device:TPU:1, one launch (start us, length us, event | category | flops | bytes accessed | tf_op | source)
XLA Modules:
  0.0 44.9 jit_solution(7658340977826558761)
XLA Ops:
  0.0 41.4 %shard_map.55 = (bf16[8,256,256]{2,1,0:T(8,128)(2,1)S(1)}, bf16[8,2,128,128]{3,2,1,0:T(8,128)(2,1)S(1)}, bf16[8,128,128]{2,1,0:T(8,128)(2,1)S(1)}) custom-call(bf16[2,3,64,128]{3,2,1,0:T(8,128)(2,1)} %bitcast.10, s32[3,8]{1,0:T(4,128)} %bitcast.11, s32[4]{0:T(128)} %sources_hbm.1, s32[2,2,3]{2,1,0:T(2,128)} %bitcast.12, bf16[4,16,2,4096]{3,2,1,0:T(2,128)(2,1)} %bitcast.9), custom_call_target="tpu_custom_call" | custom-call | tf_op jit(solution)/shard_map/pallas_call | solution.py:338
  41.4 3.5 %shard_map.56 = f32[64,64,128]{2,1,0:T(8,128)} custom-call(bf16[8,256,256]{2,1,0:T(8,128)(2,1)S(1)} %get-tuple-element.8.rows_ref, bf16[8,2,128,128]{3,2,1,0:T(8,128)(2,1)S(1)} %get-tuple-element.9.second_op_ref, bf16[8,128,128]{2,1,0:T(8,128)(2,1)S(1)} %get-tuple-element.10.third_op_ref), custom_call_target="tpu_custom_call" | custom-call | tf_op jit(solution)/shard_map/pallas_call | solution.py:402

commit v4 on v3

--- a/solution.py
+++ b/solution.py
@@ -14,7 +14,6 @@
 NX, NZ, NC = 4, 8, 2
 NY = 4
 HALF = NZ // 2
-PER_STEP = 2
 
 
 def place():
@@ -32,6 +31,15 @@
     arrived, wide, full, first_op, mom_ref, sources_ref, spins_ref, small_sem, own_sem, ring_send, ring_recv, core_send, core_recv, sum_send, sum_recv,
     share_send, share_recv, swap_send, swap_recv, per_send, per_recv, per_own,
 ):
+    own = pltpu.make_async_copy(vec_ref, fields.at[0], own_sem)
+    own.start()
+    small = [
+        pltpu.make_async_copy(mom_hbm, mom_ref, small_sem.at[0]),
+        pltpu.make_async_copy(sources_hbm, sources_ref, small_sem.at[1]),
+        pltpu.make_async_copy(spins_hbm, spins_ref, small_sem.at[2]),
+    ]
+    for copy in small:
+        copy.start()
     x, z, c = place()
     y = lax.axis_index("tpair")
     zhalf, zz = lax.div(z, HALF), lax.rem(z, HALF)
@@ -47,15 +55,6 @@
     greeted = [on_right, on_left, partner] + across + along + sinks
     for target in greeted:
         pl.semaphore_signal(barrier, inc=1, device_id=target, device_id_type=MESH)
-    own = pltpu.make_async_copy(vec_ref, fields.at[0], own_sem)
-    own.start()
-    small = [
-        pltpu.make_async_copy(mom_hbm, mom_ref, small_sem.at[0]),
-        pltpu.make_async_copy(sources_hbm, sources_ref, small_sem.at[1]),
-        pltpu.make_async_copy(spins_hbm, spins_ref, small_sem.at[2]),
-    ]
-    for copy in small:
-        copy.start()
     pl.semaphore_wait(barrier, len(greeted))
     own.wait()
 
@@ -65,16 +64,16 @@
             device_id=device, device_id_type=MESH,
         )
 
-    def ring_copy(rel, part, rightward):
+    def ring_copy(rel, piece, rightward):
         there = (rel + NZ - 1) % NZ if rightward else (rel + 1) % NZ
         return remote(
-            fields.at[rel, part], fields.at[there, part], ring_send, ring_recv.at[there, part],
+            fields.at[rel, piece // 3, piece % 3], fields.at[there, piece // 3, piece % 3], ring_send, ring_recv.at[there, piece],
             on_right if rightward else on_left,
         )
 
-    for part in range(2):
-        ring_copy(0, part, True).start()
-        ring_copy(0, part, False).start()
+    for piece in range(6):
+        ring_copy(0, piece, True).start()
+        ring_copy(0, piece, False).start()
 
     for step in range(1, NY):
         remote(per_ref.at[lax.rem(y + step, NY)], arrived.at[y], per_send, per_recv, sinks[step - 1]).start()
@@ -82,17 +81,17 @@
     per_local.start()
 
     def relay(step):
-        for part in range(2):
-            if step < HALF or part == 0:
+        for piece in range(6):
+            if step < HALF or piece < 3:
                 rel = NZ - step
-                remote(fields.at[rel, part], fields.at[rel, part], ring_send, ring_recv.at[rel, part], on_right).wait_recv()
-                if step < HALF - 1 or (step == HALF - 1 and part == 0):
-                    ring_copy(rel, part, True).start()
-            if step < HALF or part == 1:
+                remote(fields.at[rel, piece // 3, piece % 3], fields.at[rel, piece // 3, piece % 3], ring_send, ring_recv.at[rel, piece], on_right).wait_recv()
+                if step < HALF - 1 or (step == HALF - 1 and piece < 3):
+                    ring_copy(rel, piece, True).start()
+            if step < HALF or piece >= 3:
                 rel = step
-                remote(fields.at[rel, part], fields.at[rel, part], ring_send, ring_recv.at[rel, part], on_left).wait_recv()
-                if step < HALF - 1 or (step == HALF - 1 and part == 1):
-                    ring_copy(rel, part, False).start()
+                remote(fields.at[rel, piece // 3, piece % 3], fields.at[rel, piece // 3, piece % 3], ring_send, ring_recv.at[rel, piece], on_left).wait_recv()
+                if step < HALF - 1 or (step == HALF - 1 and piece >= 3):
+                    ring_copy(rel, piece, False).start()
 
     for copy in small:
         copy.wait()
@@ -181,9 +180,6 @@
             all_chunks.at[group, owner], swap_send, swap_recv.at[group], partner,
         )
 
-    per_local.wait()
-    remote(per_ref.at[0:3], arrived.at[0:3], per_send, per_recv, sinks[0]).wait()
-
     low = lax.broadcasted_iota(jnp.int32, (32, 128), 1) < 64
     even = lax.broadcasted_iota(jnp.int32, (32, 128), 1) % 2 == 0
     row = lax.broadcasted_iota(jnp.int32, (16, 128), 0)
@@ -249,8 +245,6 @@
         ).astype(jnp.bfloat16)
         return carry
 
-    lax.fori_loop(0, 2, operators, 0)
-
     for group in range(4):
         remote(core_in.at[group], core_in.at[group], core_send, core_recv.at[group], partner).wait_recv()
         for step in (2, 1, 3):
@@ -261,7 +255,9 @@
             ).start()
         own_sum[group] = total[c, group, x] + core_in[group, x]
 
-    lax.fori_loop(2, 5, operators, 0)
+    per_local.wait()
+    remote(per_ref.at[0:3], arrived.at[0:3], per_send, per_recv, sinks[0]).wait()
+    lax.fori_loop(0, 4, operators, 0)
 
     for group in range(4):
         remote(inbox.at[group], inbox.at[group], sum_send, sum_recv.at[group], across[0]).wait_recv()
@@ -276,7 +272,7 @@
         swap_copy(group, 0).start()
         all_chunks[group, slot_q] = chunk[group]
 
-    lax.fori_loop(5, 8, operators, 0)
+    lax.fori_loop(4, 8, operators, 0)
     full[pl.ds(0, 32, stride=129), :] = jnp.zeros((32, 128), jnp.float32)
     full[pl.ds(96, 32, stride=129), :] = jnp.zeros((32, 128), jnp.float32)
 
@@ -365,7 +361,7 @@
             pltpu.SMEM((3, 8), jnp.int32),
             pltpu.SMEM((4,), jnp.int32),
             pltpu.SMEM((2, 2, 3), jnp.int32),
-            dma((3,)), dma(()), dma(()), dma((NZ, 2)), dma(()), dma((4,)), dma(()), dma((4,)),
+            dma((3,)), dma(()), dma(()), dma((NZ, 6)), dma(()), dma((4,)), dma(()), dma((4,)),
             dma(()), dma((4, 3)), dma(()), dma((4,)), dma(()), dma(()), dma(()),
         ],
         compiler_params=pltpu.CompilerParams(
@@ -374,9 +370,10 @@
     )(*[pltpu.with_memory_space_constraint(value, pltpu.HBM) for value in (vecs, momenta, sources, spins, perams)])
 
 
-def contract_kernel(rows_ref, second_op_ref, third_op_ref, out_ref, second):
+def contract_kernel(rows_ref, second_op_ref, third_op_ref, out_ref, second, held, out_sem):
     keep = lax.broadcasted_iota(jnp.int32, (64, 128), 1) < 64
-    for which in range(PER_STEP):
+    copies = []
+    for which in range(8):
         kreal, kimag = second_op_ref[which, 0], second_op_ref[which, 1]
         operator = jnp.concatenate(
             [jnp.concatenate([kreal, kimag], axis=1), jnp.concatenate([-kimag, kreal], axis=1)], axis=0
@@ -384,7 +381,7 @@
         product = jnp.dot(rows_ref[which], operator, preferred_element_type=jnp.float32)
         for part in range(2):
             second[which, part] = product[:, part * 128 : (part + 1) * 128]
-    for which in range(PER_STEP):
+    for which in range(8):
         columns = []
         for i in range(8):
             parts = []
@@ -395,24 +392,27 @@
         both = jnp.dot(third_op_ref[which], jnp.concatenate(columns, axis=1), preferred_element_type=jnp.float32)
         for i in range(8):
             lanes = slice(i * 128, (i + 1) * 128)
-            out_ref[which * 8 + i] = jnp.where(keep, both[:64, lanes], both[64:, lanes])
+            held[which * 8 + i] = jnp.where(keep, both[:64, lanes], both[64:, lanes])
+        here = pl.ds(which * 8, 8)
+        copies.append(pltpu.make_async_copy(held.at[here], out_ref.at[here], out_sem.at[which]))
+        copies[-1].start()
+    for copy in copies:
+        copy.wait()
 
 
 def last_contractions(rows, second_op, third_op):
+    vmem = pl.BlockSpec(memory_space=pltpu.VMEM)
     return pl.pallas_call(
         contract_kernel,
-        grid=(8 // PER_STEP,),
         out_shape=jax.ShapeDtypeStruct((64, 64, 128), jnp.float32),
-        in_specs=[
-            pl.BlockSpec((PER_STEP, 256, 256), lambda s: (s, 0, 0)),
-            pl.BlockSpec((PER_STEP, 2, 128, 128), lambda s: (s, 0, 0, 0)),
-            pl.BlockSpec((PER_STEP, 128, 128), lambda s: (s, 0, 0)),
+        in_specs=[vmem, vmem, vmem],
+        out_specs=pl.BlockSpec(memory_space=pltpu.HBM),
+        scratch_shapes=[
+            pltpu.VMEM((8, 2, 256, 128), jnp.float32),
+            pltpu.VMEM((64, 64, 128), jnp.float32),
+            pltpu.SemaphoreType.DMA((8,)),
         ],
-        out_specs=pl.BlockSpec((8 * PER_STEP, 64, 128), lambda s: (s, 0, 0)),
-        scratch_shapes=[pltpu.VMEM((PER_STEP, 2, 256, 128), jnp.float32)],
-        compiler_params=pltpu.CompilerParams(
-            dimension_semantics=("arbitrary",), vmem_limit_bytes=16 << 20
-        ),
+        compiler_params=pltpu.CompilerParams(vmem_limit_bytes=16 << 20),
     )(rows, second_op, third_op)
 
 

time: 45 us -> 43 us (0.956)
  Pallas kernels: 44.9 us -> 42.9 us
    pallas_call x1, Pallas kernels: 3.48 us -> 2.14 us  [last_contractions(): pl.pallas_call(contract_kernel, out_shape=jax.ShapeDtypeStruct((64, 64, 1...]
    pallas_call x1, Pallas kernels: 41.4 us -> 40.8 us  [first_contraction(): pl.pallas_call(elemental_kernel, out_shape=(jax.ShapeDtypeStruct((8, 256,...]
where the time goes in v4:
time: 43 us; the launch traced here: 42.9 us
  Pallas kernels  42.9 us (100%)
    pallas_call x1, Pallas kernels, first_contraction(): pl.pallas_call(elemental_kernel, out_shape=(jax.ShapeDtypeStruct((8, 256,...  40.8 us
    pallas_call x1, Pallas kernels, last_contractions(): pl.pallas_call(contract_kernel, out_shape=jax.ShapeDtypeStruct((64, 64, 1...  2.14 us

profile of v4, /device:TPU:1, one launch (start us, length us, event | category | flops | bytes accessed | tf_op | source)
XLA Modules:
  0.0 42.9 jit_solution(9104326092042598324)
XLA Ops:
  0.0 40.8 %shard_map.55 = (bf16[8,256,256]{2,1,0:T(8,128)(2,1)S(1)}, bf16[8,2,128,128]{3,2,1,0:T(8,128)(2,1)S(1)}, bf16[8,128,128]{2,1,0:T(8,128)(2,1)S(1)}) custom-call(bf16[2,3,64,128]{3,2,1,0:T(8,128)(2,1)} %bitcast.10, s32[3,8]{1,0:T(4,128)} %bitcast.11, s32[4]{0:T(128)} %sources_hbm.1, s32[2,2,3]{2,1,0:T(2,128)} %bitcast.12, bf16[4,16,2,4096]{3,2,1,0:T(2,128)(2,1)} %bitcast.9), custom_call_target="tpu_custom_call" | custom-call | tf_op jit(solution)/shard_map/pallas_call | solution.py:334
  40.8 2.1 %shard_map.56 = f32[64,64,128]{2,1,0:T(8,128)} custom-call(bf16[8,256,256]{2,1,0:T(8,128)(2,1)S(1)} %get-tuple-element.8.rows_ref, bf16[8,2,128,128]{3,2,1,0:T(8,128)(2,1)S(1)} %get-tuple-element.9.second_op_ref, bf16[8,128,128]{2,1,0:T(8,128)(2,1)S(1)} %get-tuple-element.10.third_op_ref), custom_call_target="tpu_custom_call" | custom-call | tf_op jit(solution)/shard_map/pallas_call | solution.py:405

commit v5 on v4

--- a/solution.py
+++ b/solution.py
@@ -73,25 +73,24 @@
 
     for piece in range(6):
         ring_copy(0, piece, True).start()
-        ring_copy(0, piece, False).start()
+        ring_copy(0, (piece + 3) % 6, False).start()
 
     for step in range(1, NY):
         remote(per_ref.at[lax.rem(y + step, NY)], arrived.at[y], per_send, per_recv, sinks[step - 1]).start()
     per_local = pltpu.make_async_copy(per_ref.at[y], arrived.at[y], per_own)
     per_local.start()
 
-    def relay(step):
-        for piece in range(6):
-            if step < HALF or piece < 3:
-                rel = NZ - step
-                remote(fields.at[rel, piece // 3, piece % 3], fields.at[rel, piece // 3, piece % 3], ring_send, ring_recv.at[rel, piece], on_right).wait_recv()
-                if step < HALF - 1 or (step == HALF - 1 and piece < 3):
-                    ring_copy(rel, piece, True).start()
-            if step < HALF or piece >= 3:
-                rel = step
-                remote(fields.at[rel, piece // 3, piece % 3], fields.at[rel, piece // 3, piece % 3], ring_send, ring_recv.at[rel, piece], on_left).wait_recv()
-                if step < HALF - 1 or (step == HALF - 1 and piece >= 3):
-                    ring_copy(rel, piece, False).start()
+    def relay(step, late):
+        for count in range(3):
+            for rightward in (True, False):
+                piece = count + 3 * (late if rightward else 1 - late)
+                if step == HALF and late:
+                    continue
+                rel = NZ - step if rightward else step
+                here = fields.at[rel, piece // 3, piece % 3]
+                remote(here, here, ring_send, ring_recv.at[rel, piece], on_right if rightward else on_left).wait_recv()
+                if step < HALF - 1 or (step == HALF - 1 and not late):
+                    ring_copy(rel, piece, rightward).start()
 
     for copy in small:
         copy.wait()
@@ -116,6 +115,21 @@
                 values = fields[rel, part, colour].astype(jnp.float32)
                 vfloat[part, colour, 0:64] = values
                 vfloat[part, colour, 64:128] = values
+        at = pl.ds(rel, 1)
+        for colour in range(3):
+            for odd in range(2):
+                rows = pl.ds(odd, 32, stride=2)
+                vr, vi = vfloat[0, colour, rows], vfloat[1, colour, rows]
+                for mom in range(4):
+                    cosine, sine = cosines[mom, at, :], sines[mom, at, :]
+                    pr = (cosine * vr + sine * vi).astype(jnp.bfloat16)
+                    pi = (cosine * vi - sine * vr).astype(jnp.bfloat16)
+                    upper, lower = pl.ds(mom * 128 + odd * 32, 32), pl.ds(mom * 128 + 64 + odd * 32, 32)
+                    first, second = pl.ds(colour * 128, 128), pl.ds((3 + colour) * 128, 128)
+                    right[upper, first] = pr
+                    right[upper, second] = -pi
+                    right[lower, first] = pi
+                    right[lower, second] = pr
         for colour in range(3):
             nxt, aft = (colour + 1) % 3, (colour + 2) % 3
             for odd in range(2):
@@ -132,21 +146,6 @@
                         where = pl.ds(core * 256 + group * 64 + odd * 32, 32)
                         left[where, colour * 128 : (colour + 1) * 128] = real.astype(jnp.bfloat16)
                         left[where, (3 + colour) * 128 : (4 + colour) * 128] = imag.astype(jnp.bfloat16)
-        at = pl.ds(rel, 1)
-        for colour in range(3):
-            for odd in range(2):
-                rows = pl.ds(odd, 32, stride=2)
-                vr, vi = vfloat[0, colour, rows], vfloat[1, colour, rows]
-                for mom in range(4):
-                    cosine, sine = cosines[mom, at, :], sines[mom, at, :]
-                    pr = (cosine * vr + sine * vi).astype(jnp.bfloat16)
-                    pi = (cosine * vi - sine * vr).astype(jnp.bfloat16)
-                    upper, lower = pl.ds(mom * 128 + odd * 32, 32), pl.ds(mom * 128 + 64 + odd * 32, 32)
-                    first, second = pl.ds(colour * 128, 128), pl.ds((3 + colour) * 128, 128)
-                    right[upper, first] = pr
-                    right[upper, second] = -pi
-                    right[lower, first] = pi
-                    right[lower, second] = pr
         product = lax.dot_general(
             left[...], right[...], (((1,), (1,)), ((), ())), preferred_element_type=jnp.float32
         )
@@ -158,8 +157,8 @@
 
     def body(n, carry):
         contract(jnp.where(n % 2 == 1, NZ - (n + 1) // 2, n // 2))
-        for after, step in ((0, 1), (1, 2), (3, 3), (5, 4)):
-            pl.when(n == after)(functools.partial(relay, step))
+        for after, step, late in ((0, 1, 0), (0, 1, 1), (1, 2, 0), (1, 2, 1), (3, 3, 0), (4, 3, 1), (6, 4, 0)):
+            pl.when(n == after)(functools.partial(relay, step, late))
         return carry
 
     lax.fori_loop(0, NZ, body, 0)

time: 43 us -> 40.4 us (0.940)
  Pallas kernels: 42.9 us -> 40.4 us
    pallas_call x1, Pallas kernels: 40.8 us -> 38.2 us  [first_contraction(): pl.pallas_call(elemental_kernel, out_shape=(jax.ShapeDtypeStruct((8, 256,...]
where the time goes in v5:
time: 40.4 us
  Pallas kernels  40.4 us (100%)
    pallas_call x1, Pallas kernels, first_contraction(): pl.pallas_call(elemental_kernel, out_shape=(jax.ShapeDtypeStruct((8, 256,...  38.2 us
    pallas_call x1, Pallas kernels, last_contractions(): pl.pallas_call(contract_kernel, out_shape=jax.ShapeDtypeStruct((64, 64, 1...  2.14 us

profile of v5, /device:TPU:1, one launch (start us, length us, event | category | flops | bytes accessed | tf_op | source)
XLA Modules:
  0.0 40.4 jit_solution(11272747114553966981)
XLA Ops:
  0.0 38.2 %shard_map.55 = (bf16[8,256,256]{2,1,0:T(8,128)(2,1)S(1)}, bf16[8,2,128,128]{3,2,1,0:T(8,128)(2,1)S(1)}, bf16[8,128,128]{2,1,0:T(8,128)(2,1)S(1)}) custom-call(bf16[2,3,64,128]{3,2,1,0:T(8,128)(2,1)} %bitcast.10, s32[3,8]{1,0:T(4,128)} %bitcast.11, s32[4]{0:T(128)} %sources_hbm.1, s32[2,2,3]{2,1,0:T(2,128)} %bitcast.12, bf16[4,16,2,4096]{3,2,1,0:T(2,128)(2,1)} %bitcast.9), custom_call_target="tpu_custom_call" | custom-call | tf_op jit(solution)/shard_map/pallas_call | solution.py:333
  38.2 2.1 %shard_map.56 = f32[64,64,128]{2,1,0:T(8,128)} custom-call(bf16[8,256,256]{2,1,0:T(8,128)(2,1)S(1)} %get-tuple-element.8.rows_ref, bf16[8,2,128,128]{3,2,1,0:T(8,128)(2,1)S(1)} %get-tuple-element.9.second_op_ref, bf16[8,128,128]{2,1,0:T(8,128)(2,1)S(1)} %get-tuple-element.10.third_op_ref), custom_call_target="tpu_custom_call" | custom-call | tf_op jit(solution)/shard_map/pallas_call | solution.py:404

commit v6 on v5

--- a/solution.py
+++ b/solution.py
@@ -109,7 +109,7 @@
 
     total[...] = jnp.zeros_like(total)
 
-    def contract(rel):
+    def build(rel, slot):
         for part in range(2):
             for colour in range(3):
                 values = fields[rel, part, colour].astype(jnp.float32)
@@ -126,10 +126,10 @@
                     pi = (cosine * vi - sine * vr).astype(jnp.bfloat16)
                     upper, lower = pl.ds(mom * 128 + odd * 32, 32), pl.ds(mom * 128 + 64 + odd * 32, 32)
                     first, second = pl.ds(colour * 128, 128), pl.ds((3 + colour) * 128, 128)
-                    right[upper, first] = pr
-                    right[upper, second] = -pi
-                    right[lower, first] = pi
-                    right[lower, second] = pr
+                    right[slot, upper, first] = pr
+                    right[slot, upper, second] = -pi
+                    right[slot, lower, first] = pi
+                    right[slot, lower, second] = pr
         for colour in range(3):
             nxt, aft = (colour + 1) % 3, (colour + 2) % 3
             for odd in range(2):
@@ -144,10 +144,11 @@
                         real = lrn * rra - lin * ria - (lra * rrn - lia * rin)
                         imag = lrn * ria + lin * rra - (lra * rin + lia * rrn)
                         where = pl.ds(core * 256 + group * 64 + odd * 32, 32)
-                        left[where, colour * 128 : (colour + 1) * 128] = real.astype(jnp.bfloat16)
-                        left[where, (3 + colour) * 128 : (4 + colour) * 128] = imag.astype(jnp.bfloat16)
+                        left[slot, where, colour * 128 : (colour + 1) * 128] = real.astype(jnp.bfloat16)
+                        left[slot, where, (3 + colour) * 128 : (4 + colour) * 128] = imag.astype(jnp.bfloat16)
+    def multiply(slot):
         product = lax.dot_general(
-            left[...], right[...], (((1,), (1,)), ((), ())), preferred_element_type=jnp.float32
+            left[slot], right[slot], (((1,), (1,)), ((), ())), preferred_element_type=jnp.float32
         )
         for core in range(2):
             for group in range(4):
@@ -155,13 +156,22 @@
                 for mom in range(4):
                     total[core, group, mom] += product[at : at + 64, mom * 128 : (mom + 1) * 128]
 
-    def body(n, carry):
-        contract(jnp.where(n % 2 == 1, NZ - (n + 1) // 2, n // 2))
-        for after, step, late in ((0, 1, 0), (0, 1, 1), (1, 2, 0), (1, 2, 1), (3, 3, 0), (4, 3, 1), (6, 4, 0)):
-            pl.when(n == after)(functools.partial(relay, step, late))
+    left[1] = jnp.zeros_like(left[1])
+    right[1] = jnp.zeros_like(right[1])
+    schedule = ((0, 1, 0), (0, 1, 1), (1, 2, 0), (1, 2, 1), (3, 3, 0), (4, 3, 1), (6, 4, 0))
+
+    def body(pair, carry):
+        for slot in range(2):
+            n = 2 * pair + slot
+            build(NZ - (n + 1) // 2 if slot else n // 2, slot)
+            multiply(1 - slot)
+            for after, step, late in schedule:
+                if after % 2 == slot:
+                    pl.when(pair == after // 2)(functools.partial(relay, step, late))
         return carry
 
-    lax.fori_loop(0, NZ, body, 0)
+    lax.fori_loop(0, NZ // 2, body, 0)
+    multiply(1)
 
     for group in range(4):
         remote(total.at[1 - c, group], core_in.at[group], core_send, core_recv.at[group], partner).start()
@@ -256,7 +266,6 @@
 
     per_local.wait()
     remote(per_ref.at[0:3], arrived.at[0:3], per_send, per_recv, sinks[0]).wait()
-    lax.fori_loop(0, 4, operators, 0)
 
     for group in range(4):
         remote(inbox.at[group], inbox.at[group], sum_send, sum_recv.at[group], across[0]).wait_recv()
@@ -271,7 +280,7 @@
         swap_copy(group, 0).start()
         all_chunks[group, slot_q] = chunk[group]
 
-    lax.fori_loop(4, 8, operators, 0)
+    lax.fori_loop(0, 8, operators, 0)
     full[pl.ds(0, 32, stride=129), :] = jnp.zeros((32, 128), jnp.float32)
     full[pl.ds(96, 32, stride=129), :] = jnp.zeros((32, 128), jnp.float32)
 
@@ -344,8 +353,8 @@
             pltpu.VMEM((4, NZ, 128), f32),
             pltpu.VMEM((NZ, 2, 3, 64, 128), bf16),
             pltpu.VMEM((2, 3, 128, 128), f32),
-            pltpu.VMEM((512, 768), bf16),
-            pltpu.VMEM((512, 768), bf16),
+            pltpu.VMEM((2, 512, 768), bf16),
+            pltpu.VMEM((2, 512, 768), bf16),
             pltpu.VMEM((2, 4, 4, 64, 128), f32),
             pltpu.VMEM((4, 4, 64, 128), f32),
             pltpu.VMEM((4, 64, 128), f32),

time: 40.4 us -> 40.8 us (level)
  no operation moved by 1% of the time
where the time goes in v6:
time: 40.8 us
  Pallas kernels  40.8 us (100%)
    pallas_call x1, Pallas kernels, first_contraction(): pl.pallas_call(elemental_kernel, out_shape=(jax.ShapeDtypeStruct((8, 256,...  38.6 us
    pallas_call x1, Pallas kernels, last_contractions(): pl.pallas_call(contract_kernel, out_shape=jax.ShapeDtypeStruct((64, 64, 1...  2.14 us

profile of v6, /device:TPU:1, one launch (start us, length us, event | category | flops | bytes accessed | tf_op | source)
XLA Modules:
  0.0 40.8 jit_solution(11983436240175315341)
XLA Ops:
  0.0 38.6 %shard_map.55 = (bf16[8,256,256]{2,1,0:T(8,128)(2,1)S(1)}, bf16[8,2,128,128]{3,2,1,0:T(8,128)(2,1)S(1)}, bf16[8,128,128]{2,1,0:T(8,128)(2,1)S(1)}) custom-call(bf16[2,3,64,128]{3,2,1,0:T(8,128)(2,1)} %bitcast.10, s32[3,8]{1,0:T(4,128)} %bitcast.11, s32[4]{0:T(128)} %sources_hbm.1, s32[2,2,3]{2,1,0:T(2,128)} %bitcast.12, bf16[4,16,2,4096]{3,2,1,0:T(2,128)(2,1)} %bitcast.9), custom_call_target="tpu_custom_call" | custom-call | tf_op jit(solution)/shard_map/pallas_call | solution.py:342
  38.6 2.1 %shard_map.56 = f32[64,64,128]{2,1,0:T(8,128)} custom-call(bf16[8,256,256]{2,1,0:T(8,128)(2,1)S(1)} %get-tuple-element.8.rows_ref, bf16[8,2,128,128]{3,2,1,0:T(8,128)(2,1)S(1)} %get-tuple-element.9.second_op_ref, bf16[8,128,128]{2,1,0:T(8,128)(2,1)S(1)} %get-tuple-element.10.third_op_ref), custom_call_target="tpu_custom_call" | custom-call | tf_op jit(solution)/shard_map/pallas_call | solution.py:413
